TPU v7x, 128 devices: a whole 4x4x4 slice. The times are simulated.
128 devices in a mesh: tok: 8 (over z_lo, x), mem: 8 (over z_hi, y), row: 2 (over core).
Axes of the slice: x: 4, y: 4, z: 4 (z_hi: 2, z_lo: 2; z = z_hi * 2 + z_lo), core: 2. Of those that a mesh axis runs over, the one named last changes fastest.
Arguments:
- queries: bfloat16 [2, 4096, 8192], P(None, ('tok', 'row'), 'mem'), may hold values from -55 to 55
- keys: bfloat16 [2, 4096, 8192], P(None, ('tok', 'row'), 'mem'), may hold values from -3 to 3
- values: bfloat16 [2, 4096, 8192], P(None, ('tok', 'row'), 'mem'), may hold values from -6 to 6
- token_lr: float32 [16, 2, 4096], P('mem', None, ('tok', 'row')), may hold values from 0.05 to 0.5
- momentum_rate: float32 [16], P('mem'), may hold values from 0.3 to 0.9
- update_step: float32 [16], P('mem'), may hold values from 0.2 to 0.6
- fast_weights: float32 [16, 3, 512, 512], P('mem', None, 'row'), may hold values from -0.25 to 0.25
- momentum: float32 [16, 3, 512, 512], P('mem', None, 'row'), may hold values from -24 to 24
Outputs:
- mixed: bfloat16 [2, 4096, 8192], P(None, ('tok', 'row'), 'mem')
- new_weights: float32 [16, 3, 512, 512], P('mem', None, 'row')
- new_momentum: float32 [16, 3, 512, 512], P('mem', None, 'row')
All inputs are finite; a program needn't handle non-finite values.
Results may differ from a plain program's by a relative error of at most 0.02.
Values may be sent and summed in bfloat16 or wider, within the bound.
A program may use at most 128 MiB of HBM per device.

v0:
```python
import jax
import jax.numpy as jnp
from jax import lax
from jax.sharding import PartitionSpec as P

DH = 512
HEAD_DIM = 128
WINDOW = 256
NS_STEPS = 2
GROUPS = 2


quintic_one = 3.4445
quintic_two = -4.775
quintic_three = 2.0315


def shifted(value, axis, steps):
    count = lax.axis_size(axis)
    pairs = [(source, (source + steps) % count) for source in range(count)]
    return lax.ppermute(value, axis, pairs)


def unit_rows(field):
    field = field.astype(jnp.float32)
    return field * lax.rsqrt(jnp.mean(field * field, axis=-1, keepdims=True) + 1e-05)


def refine(ortho, gram):
    gram_half = gram.astype(jnp.bfloat16)
    square = jnp.einsum("hmde,hmef->hmdf", gram_half, gram_half, preferred_element_type=jnp.float32)
    poly = (quintic_two * gram + quintic_three * square).astype(jnp.bfloat16)
    turned = jnp.einsum("hmrd,hmde->hmre", ortho, poly, preferred_element_type=jnp.float32)
    return (quintic_one * ortho.astype(jnp.float32) + turned).astype(jnp.bfloat16)


def sliding_attention(queries, keys, values):
    groups, local_len, local_width = queries.shape
    heads = local_width // HEAD_DIM
    tails = jnp.stack([keys, values], axis=0)
    received = shifted(tails, ("tok", "row"), 1)
    device = lax.axis_index(("tok", "row"))
    earlier = jnp.concatenate([jnp.zeros_like(received[:, :1]), received[:, :-1]], axis=1)
    halo = jnp.where(device == 0, earlier, received)
    ext_keys = jnp.concatenate([halo[0], keys], axis=1)
    ext_values = jnp.concatenate([halo[1], values], axis=1)
    block_len = min(local_len, 512)
    count = local_len // block_len
    group_total = local_len * lax.axis_size(("tok", "row"))
    scale = HEAD_DIM ** (-0.5)
    group_base = jnp.arange(groups, dtype=jnp.int32) * group_total + device * local_len

    def attend(block):
        start = block * block_len
        span = block_len + WINDOW
        query_part = queries.reshape(groups, block_len, heads, HEAD_DIM)
        key_part = ext_keys.reshape(groups, span, heads, HEAD_DIM)
        value_part = ext_values.reshape(groups, span, heads, HEAD_DIM)
        scores = (
            jnp.einsum("cqae,ckae->caqk", query_part, key_part, preferred_element_type=jnp.float32)
            * scale
        )
        query_local = start + jnp.arange(block_len, dtype=jnp.int32)
        key_local = start - WINDOW + jnp.arange(span, dtype=jnp.int32)
        offset = query_local[:, None] - key_local[None, :]
        near = (offset >= 0) & (offset < WINDOW)
        placed = group_base[:, None] + key_local[None, :] >= 0
        allowed = near[None, None, :, :] & placed[:, None, None, :]
        scores = jnp.where(allowed, scores, -1e30)
        top = jnp.max(scores, axis=-1, keepdims=True)
        expo = jnp.exp(scores - top)
        probs = (expo / jnp.sum(expo, axis=-1, keepdims=True)).astype(jnp.bfloat16)
        result = jnp.einsum(
            "caqk,ckae->cqae", probs, value_part, preferred_element_type=jnp.float32
        )
        return result.reshape(groups, block_len, local_width)

    pieces = lax.map(attend, jnp.arange(count, dtype=jnp.int32))
    return jnp.moveaxis(pieces, 0, 1).reshape(groups, local_len, local_width)


def shards(queries, keys, values, token_lr, momentum_rate, update_step, fast_weights, momentum):
    attended = sliding_attention(queries, keys, values)
    groups, local_len, local_width = queries.shape
    heads_local = local_width // DH
    query_unit = unit_rows(queries.reshape(groups, local_len, heads_local, DH)).astype(jnp.bfloat16)
    key_unit = unit_rows(keys.reshape(groups, local_len, heads_local, DH)).astype(jnp.bfloat16)
    value_heads = values.reshape(groups, local_len, heads_local, DH)
    rows = fast_weights.shape[2]
    row_start = lax.axis_index("row") * rows
    weights = fast_weights
    moment = momentum
    recalls = []
    for index in range(GROUPS):
        half = lax.all_gather(weights.astype(jnp.bfloat16), "row", axis=2, tiled=True)
        gate_w = half[:, 0]
        up_w = half[:, 1]
        down_w = half[:, 2]
        query_gate = jnp.einsum(
            "lhd,hdf->lhf", query_unit[index], gate_w, preferred_element_type=jnp.float32
        )
        query_up = jnp.einsum(
            "lhd,hdf->lhf", query_unit[index], up_w, preferred_element_type=jnp.float32
        )
        query_hidden = (jax.nn.silu(query_gate) * query_up).astype(jnp.bfloat16)
        recall = jnp.einsum(
            "lhf,hfd->lhd", query_hidden, down_w, preferred_element_type=jnp.float32
        )
        recalls.append(recall.reshape(local_len, local_width))
        key_gate = jnp.einsum(
            "lhd,hdf->lhf", key_unit[index], gate_w, preferred_element_type=jnp.float32
        )
        key_up = jnp.einsum(
            "lhd,hdf->lhf", key_unit[index], up_w, preferred_element_type=jnp.float32
        )
        key_hidden = (jax.nn.silu(key_gate) * key_up).astype(jnp.bfloat16)
        rate = jnp.transpose(token_lr[:, index, :])[:, :, None]
        target = (-(rate * value_heads[index].astype(jnp.float32))).astype(jnp.bfloat16)
        back = jnp.einsum("lhd,hfd->lhf", target, down_w, preferred_element_type=jnp.float32)
        sig = jax.nn.sigmoid(key_gate)
        gate_in = (back * key_up * sig * (1.0 + key_gate * (1.0 - sig))).astype(jnp.bfloat16)
        up_in = (back * jax.nn.silu(key_gate)).astype(jnp.bfloat16)
        gradient = jnp.stack(
            [
                jnp.einsum(
                    "lhd,lhf->hdf", key_unit[index], gate_in, preferred_element_type=jnp.float32
                ),
                jnp.einsum(
                    "lhd,lhf->hdf", key_unit[index], up_in, preferred_element_type=jnp.float32
                ),
                jnp.einsum("lhf,lhd->hfd", key_hidden, target, preferred_element_type=jnp.float32),
            ],
            axis=1,
        )
        summed = lax.psum(gradient.astype(jnp.bfloat16), ("tok", "row")).astype(jnp.float32)
        owned = lax.dynamic_slice_in_dim(summed, row_start, rows, 2)
        moment = momentum_rate[:, None, None, None] * moment + owned
        whole = lax.all_gather(moment.astype(jnp.bfloat16), "row", axis=2, tiled=True).astype(
            moment.dtype
        )
        ortho = (
            whole * lax.rsqrt(jnp.sum(whole * whole, axis=(2, 3), keepdims=True) + 1e-06)
        ).astype(jnp.bfloat16)
        for turn in range(NS_STEPS):
            gram = jnp.einsum("hmrd,hmre->hmde", ortho, ortho, preferred_element_type=jnp.float32)
            ortho = refine(ortho, gram)
        ortho = lax.dynamic_slice_in_dim(ortho, row_start, rows, 2)
        stepped = weights - update_step[:, None, None, None] * ortho.astype(jnp.float32)
        columns = lax.psum(jnp.sum(stepped * stepped, axis=2), "row")
        weights = stepped * lax.rsqrt(columns[:, :, None, :] + 1e-06)
    mixed = (attended + jnp.stack(recalls, axis=0)).astype(jnp.bfloat16)
    return (mixed, weights, moment)


def solution(mesh):
    return jax.shard_map(
        shards,
        mesh=mesh,
        in_specs=(
            P(None, ("tok", "row"), "mem"),
            P(None, ("tok", "row"), "mem"),
            P(None, ("tok", "row"), "mem"),
            P("mem", None, ("tok", "row")),
            P("mem"),
            P("mem"),
            P("mem", None, "row", None),
            P("mem", None, "row", None),
        ),
        out_specs=(
            P(None, ("tok", "row"), "mem"),
            P("mem", None, "row", None),
            P("mem", None, "row", None),
        ),
        check_vma=False,
    )
```

profile of v0, /device:TPU:1, one launch (start us, length us, event | category | flops | bytes accessed | tf_op | source)
XLA Modules:
  0.0 439.6 jit_solution(13480996230644028582)
XLA Ops:
  7.2 3.3 copy.192
  11.8 2.8 slice_convert_fusion
  14.5 3.1 reshape.149
  18.1 11.1 %all-gather.5.cloned.1.call-done = bf16[2,3,512,512]{3,2,0,1:T(8,128)(2,1)} async-done(((bf16[2,3,256,512]{3,2,0,1:T(8,128)(2,1)}), bf16[2,3,512,512]{3,2,0,1:T(8,128)(2,1)}) %all-gather.5.cloned.1.call-update) | async-done | bytes 3145744 | tf_op jit(solution)/shard_map/all_gather | solution.py:95
  29.2 1.7 convolution_bitcast_fusion.5
  30.8 1.7 convolution_bitcast_fusion.6
  33.3 1.7 convolution_bitcast_fusion.7
  35.0 0.8 fusion.59
  36.5 2.0 pad_maximum_fusion
  38.6 127.0 %all-reduce.4.cloned.1.call-done = bf16[2,3,512,512]{3,2,0,1:T(8,128)(2,1)} async-done(((bf16[2,3,512,512]{3,2,0,1:T(8,128)(2,1)}), bf16[2,3,512,512]{3,2,0,1:T(8,128)(2,1)}) %all-reduce.4.cloned.1.call-update) | async-done | bytes 3145744 | tf_op jit(solution)/shard_map/psum | solution.py:135
  165.6 3.1 fusion.58
  169.0 16.5 %all-gather.7.cloned.1.call-done = bf16[2,3,512,512]{3,2,0,1:T(8,128)(2,1)} async-done(((bf16[2,3,256,512]{3,2,0,1:T(8,128)(2,1)}), bf16[2,3,512,512]{3,2,0,1:T(8,128)(2,1)}) %all-gather.7.cloned.1.call-update) | async-done | bytes 3145744 | tf_op jit(solution)/shard_map/all_gather | solution.py:138
  185.5 2.9 fusion.2
  188.3 2.1 fusion.18
  190.5 2.0 add_convert_fusion.5
  192.5 2.0 add_convert_fusion.4
  194.5 1.8 fusion.16
  196.4 2.0 add_convert_fusion.3
  198.4 1.8 fusion.24
  200.3 1.4 multiply_reduce_fusion.1
  201.7 3.3 psum.29
  205.1 1.6 multiply_convert_fusion
  206.7 2.3 copy.55
  209.0 3.1 pad_maximum_fusion.2
  212.1 1.5 collective-permute-start
  213.6 3.1 reshape.150
  216.7 6.4 %all-gather.9.cloned.1.call-done = bf16[2,3,512,512]{3,2,0,1:T(8,128)(2,1)} async-done(((bf16[2,3,256,512]{3,2,0,1:T(8,128)(2,1)}), bf16[2,3,512,512]{3,2,0,1:T(8,128)(2,1)}) %all-gather.9.cloned.1.call-update) | async-done | bytes 3145744 | tf_op jit(solution)/shard_map/all_gather | solution.py:95
  223.1 1.9 convolution_bitcast_fusion
  225.0 1.8 convolution_bitcast_fusion.1
  227.6 1.7 convolution_bitcast_fusion.4
  230.8 2.0 pad_maximum_fusion.1
  232.9 2.3 copy.62
  235.2 2.3 copy.59
  237.5 2.6 copy.63
  240.1 1.4 multiply_reduce_fusion.3
  242.0 2.9 multiply_convert_fusion.2
  244.9 1.3 slice.78
  246.2 1.8 pad_select_fusion
  248.0 1.5 fusion.115
  249.5 2.3 copy.58
  251.7 6.4 %fusion.52 = f32[2,8,512,256]{3,2,1,0:T(8,128)} fusion(bf16[2,256,8,128]{3,1,2,0:T(8,128)(2,1)} %copy.59, bf16[2,256,8,128]{3,1,2,0:T(8,128)(2,1)} %copy.58, bf16[2,256,1024]{2,1,0:T(8,128)(2,1)} %param.8), kind=kOutput, calls=%fused_computation.66 | convolution fusion | flops 541065216 | bytes 11534336 | tf_op jit(solution)/shard_map/while/body/eval_jaxpr/cqae,ckae->caqk/dot_general | solution.py:60
  258.1 101.8 %all-reduce.6.cloned.1.call-done = bf16[2,3,512,512]{3,2,0,1:T(8,128)(2,1)} async-done(((bf16[2,3,512,512]{3,2,0,1:T(8,128)(2,1)}), bf16[2,3,512,512]{3,2,0,1:T(8,128)(2,1)}) %all-reduce.6.cloned.1.call-update) | async-done | bytes 3145744 | tf_op jit(solution)/shard_map/psum | solution.py:135
  359.9 5.9 %fusion.114 = (bf16[2,3,256,512]{3,2,0,1:T(8,128)(2,1)}, f32[2,3,256,512]{3,2,0,1:T(8,128)}) fusion(bf16[2,3,512,512]{3,2,0,1:T(8,128)(2,1)} %all-reduce.6.cloned.1.call-done, s32[]{:T(128)S(6)} %select_n.22, bf16[2,3,512,512]{3,2,0,1:T(8,128)(2,1)} %all-reduce.4.cloned.1.call-done, f32[2,3,256,512]{3,2,1,0:T(8,128)} %param.15, f32[2]{0:T(128)S(1)} %copy-done.15), kind=kLoop, calls=%fused_computation.177 | loop fusion | flops 5505024 | bytes 11010060 | tf_op jit(solution)/shard_map/convert_element_type | solution.py:138
  365.9 9.4 %fusion.117 = (f32[2,8,256]{2,1,0:T(8,128)S(1)}, f32[2,8,256,512]{2,3,1,0:T(8,128)S(1)}) fusion(f32[2,8,512,256]{3,2,1,0:T(8,128)} %fusion.52, pred[2,256,512]{1,2,0:T(8,128)(4,1)S(1)} %broadcast_and_fusion), kind=kOutput, calls=%fused_computation.180 | output fusion | flops 12583423 | bytes 17055744 | tf_op jit(solution)/shard_map/while/body/eval_jaxpr/sub | solution.py:71
  375.3 2.1 fusion.8
  377.4 2.9 convolution_bitcast_fusion.10
  380.3 3.7 convolution_bitcast_fusion.8
  384.0 2.6 copy.65
  386.6 2.8 convolution_bitcast_fusion.3
  389.4 4.0 fusion.69
  393.4 3.4 fusion.56
  396.9 2.4 copy.102
  399.3 4.1 copy.104
  403.4 2.9 fusion.4
  406.3 2.2 fusion.14
  408.5 3.7 add_convert_fusion.2
  412.2 3.9 add_convert_fusion.1
  416.1 1.8 fusion.12
  418.0 2.0 add_convert_fusion
  420.0 1.8 fusion.20
  421.8 2.3 multiply_reduce_fusion
  424.2 4.3 psum.31
  428.5 2.1 fusion.57
  430.6 2.0 copy.103
  (69 shorter events, 6.3 us)
Async XLA Ops:
  7.2 3.5 copy-start.14
  7.2 3.5 copy-start.11
  7.2 22.0 %all-gather.5.cloned.1.call-start = ((), (), s32[]{:S(2)}) async-start(), calls=%async_computation | async-start | bytes 4718592 | tf_op jit(solution)/shard_map/all_gather | solution.py:95
  10.6 155.0 %all-reduce.4.cloned.1.call-start = ((), (), s32[]{:S(2)}) async-start(), calls=%async_computation.1 | async-start | bytes 6291456 | tf_op jit(solution)/shard_map/psum | solution.py:135
  11.2 6.4 %copy-start = (bf16[2,256,1024]{1,2,0:T(8,128)(2,1)}, bf16[2,256,1024]{1,2,0:T(8,128)(2,1)S(1)}, u32[]{:S(2)}) copy-start(bf16[2,256,1024]{1,2,0:T(8,128)(2,1)S(1)} %copy.54) | copy-start | bytes 3145732
  18.1 17.8 %copy-start.3 = (bf16[2,256,2,512]{3,1,2,0:T(8,128)(2,1)}, bf16[2,256,2,512]{3,1,2,0:T(8,128)(2,1)S(1)}, u32[]{:S(2)}) copy-start(bf16[2,256,2,512]{3,1,2,0:T(8,128)(2,1)S(1)} %multiply_convert_fusion.1) | copy-start | bytes 3145732
  18.1 14.4 %copy-start.7 = (f32[256,2,512]{2,1,0:T(2,128)S(1)}, f32[256,2,512]{2,1,0:T(2,128)}, u32[]{:S(2)}) copy-start(f32[256,2,512]{2,1,0:T(2,128)} %reshape.149) | copy-start | bytes 3145732
  38.5 127.1 %copy-start.2 = (f32[2,3,256,512]{3,2,1,0:T(8,128)S(1)}, f32[2,3,256,512]{3,2,1,0:T(8,128)}, u32[]{:S(2)}) copy-start(f32[2,3,256,512]{3,2,1,0:T(8,128)} %param.15) | copy-start | bytes 9437188
  38.5 127.1 %copy-start.15 = (f32[2]{0:T(128)S(1)}, f32[2]{0:T(128)}, u32[]{:S(2)}) copy-start(f32[2]{0:T(128)} %param.12) | copy-start | bytes 28
  38.5 146.9 %all-gather.7.cloned.1.call-start = ((), (), s32[]{:S(2)}) async-start(), calls=%async_computation.2 | async-start | bytes 4718592 | tf_op jit(solution)/shard_map/all_gather | solution.py:138
  168.7 54.4 %all-gather.9.cloned.1.call-start = ((), (), s32[]{:S(2)}) async-start(), calls=%async_computation.3 | async-start | bytes 4718592 | tf_op jit(solution)/shard_map/all_gather | solution.py:95
  185.5 2.9 copy-start.10
  198.4 1.9 copy-start.1
  198.4 1.9 copy-start.13
  206.7 153.2 %all-reduce.6.cloned.1.call-start = ((), (), s32[]{:S(2)}) async-start(), calls=%async_computation.4 | async-start | bytes 6291456 | tf_op jit(solution)/shard_map/psum | solution.py:135
  212.1 32.8 %collective-permute-start = (bf16[2,2,256,1024]{2,3,1,0:T(8,128)(2,1)}, bf16[2,2,256,1024]{2,3,1,0:T(8,128)(2,1)}, u32[]{:S(2)}, u32[]{:S(2)}) collective-permute-start(bf16[2,2,256,1024]{2,3,1,0:T(8,128)(2,1)} %pad_maximum_fusion.2), channel_id=1, source_target_pairs={{0,1},{1,16},{16,17},{17,32},{32,33},{33,48},{48,49},{49,64},{64,6... | collective-permute-start | bytes 6291464 | tf_op jit(solution)/shard_map/ppermute | solution.py:21
  223.1 3.7 copy-start.8
  226.8 2.6 copy-start.4
  232.9 170.6 %all-gather.11.cloned.1.call-start = ((), (), s32[]{:S(2)}) async-start(), calls=%async_computation.5 | async-start | bytes 4718592 | tf_op jit(solution)/shard_map/all_gather | solution.py:138
  365.9 9.4 %copy-start.6 = (bf16[2,256,1024]{1,2,0:T(8,128)(2,1)S(1)}, bf16[2,256,1024]{1,2,0:T(8,128)(2,1)}, u32[]{:S(2)}) copy-start(bf16[2,256,1024]{1,2,0:T(8,128)(2,1)} %copy.55) | copy-start | bytes 3145732
  365.9 9.4 %copy-start.12 = (bf16[1,2,256,1024]{2,3,1,0:T(8,128)(2,1)S(1)}, bf16[1,2,256,1024]{2,3,1,0:T(8,128)(2,1)}, u32[]{:S(2)}) copy-start(bf16[1,2,256,1024]{2,3,1,0:T(8,128)(2,1)} %get-tuple-element.33) | copy-start | bytes 3145732
  375.3 2.1 copy-start.5
  403.4 2.9 copy-start.9
Sparse Core Ops, SparseCore 0:
  10.7 18.4 all-gather.4
  38.6 126.8 all-reduce.3
  168.8 16.5 all-gather.6
  206.8 16.2 all-gather.8
  233.0 126.8 all-reduce.5
  366.0 16.5 all-gather.10
where the time goes:
time: 446 us; the launch traced here: 440 us
  waiting for transfers between devices  263 us (59%)
  matrix products  64.1 us (14%)
  other arithmetic  52 us (12%)
  local copies, waits for them, and re-layouts  36.3 us (8%)
  between operations  14.7 us (3%)
  blocking collectives  7.62 us (2%)
    psum x2, waiting for transfers between devices, shards(): lax.psum(gradient.astype(jnp.bfloat16), ('tok', 'row')).astype(jnp.float32)  229 us
    all_gather x2, waiting for transfers between devices, shards(): lax.all_gather(weights.astype(jnp.bfloat16), 'row', axis=2, tiled=True)  17.5 us
    unnamed x41, local copies, waits for them, and re-layouts  17 us
    all_gather x2, waiting for transfers between devices, shards(): lax.all_gather(moment.astype(jnp.bfloat16), 'row', axis=2, tiled=True)  16.5 us
    dot_general x4, matrix products, refine(): jnp.einsum('hmde,hmef->hmdf', gram_half, gram_half, preferred_element_typ...  9.87 us
    dot_general x4, matrix products, refine(): jnp.einsum('hmrd,hmde->hmre', ortho, poly, preferred_element_type=jnp.flo...  9.54 us
    sub x1, other arithmetic, attend(): expo = jnp.exp(scores - top)  9.43 us
    convert_element_type x2, other arithmetic, shards(): moment.astype(jnp.bfloat16)  9.06 us
  transfers between devices with their start and end apart: 7, of which 5 were waited for; matrix products, arithmetic and copies ran while one was open for 20% of the time, Pallas kernels for 0%

commit v1 on v0

v1 whole, which is shorter than its diff:
```python
import jax
import jax.numpy as jnp
from jax import lax
from jax.experimental import pallas as pl
from jax.experimental.pallas import tpu as pltpu
from jax.sharding import PartitionSpec as P

DH = 512
HEAD_DIM = 128
QUINTIC = (3.4445, -4.775, 2.0315)
MESH = pl.DeviceIdType.MESH
F32 = jnp.float32
BF16 = jnp.bfloat16
T = 256
UNITS = 12


def dot(a, b, dims=((1,), (0,))):
    return lax.dot_general(a, b, (dims, ((), ())), preferred_element_type=F32)


def unit_rows(field):
    field = field.astype(F32)
    return (field * lax.rsqrt(jnp.mean(field * field, axis=-1, keepdims=True) + 1e-05)).astype(BF16)


def kernel(
    q_in, k_in, v_in, lr_in, rate_in, step_in, w_in, m_in,
    mixed_out, w_out, m_out,
    qv, kv, vv, halo, mix, recall, w32, m32, w16, m_send, m_recv,
    left, right, send_a, recv_a, own, send_b, recv_b1, send_b2, recv_b2, total,
    ortho, gram, gram16, poly,
    load_sem, w_load, m_load, w_ssem, w_rsem, m_ssem, m_rsem, h_ssem, h_rsem,
    ssem, rsem, out_sem, mix_sem,
):
    tok = lax.axis_index("tok")
    row = lax.axis_index("row")
    x = lax.rem(tok, 4)
    z = lax.div(tok, 4)
    other = 1 - row
    z_tok = lax.rem(tok + 4, 8)
    device = tok * 2 + row
    after = lax.rem(device + 1, 16)
    before = lax.rem(device + 15, 16)
    mine = pl.multiple_of(row * T, T)
    theirs = pl.multiple_of(other * T, T)

    def chip(t):
        return {"tok": t, "row": row}

    partner = {"tok": tok, "row": other}
    z_peer = chip(z_tok)
    next_dev = {"tok": lax.div(after, 2), "row": lax.rem(after, 2)}
    prev_dev = {"tok": lax.div(before, 2), "row": lax.rem(before, 2)}

    def x_of(k):
        return lax.rem(x + k, 4)

    def x_peer(k):
        return chip(z * 4 + x_of(k))

    def remote(src, dst, send, recv, target):
        return pltpu.make_async_remote_copy(
            src_ref=src, dst_ref=dst, send_sem=send, recv_sem=recv,
            device_id=target, device_id_type=MESH,
        )

    def w_copy(i):
        return pltpu.make_async_copy(
            w_in.at[lax.div(i, 3), lax.rem(i, 3)], w32.at[i, pl.ds(mine, T)], w_load.at[i]
        )

    def m_copy(i):
        return pltpu.make_async_copy(
            m_in.at[lax.div(i, 3), lax.rem(i, 3)], m32.at[i, pl.ds(mine, T)], m_load.at[i]
        )

    k_copy = pltpu.make_async_copy(k_in, kv, load_sem.at[0])
    v_copy = pltpu.make_async_copy(v_in, vv, load_sem.at[1])
    q_copy = pltpu.make_async_copy(q_in, qv, load_sem.at[2])

    @pl.loop(0, 6)
    def _(i):
        w_copy(i).start()

    k_copy.start()
    v_copy.start()

    @pl.loop(0, 6)
    def _(i):
        m_copy(i).start()

    q_copy.start()

    barrier = pltpu.get_barrier_semaphore()
    for target in (partner, x_peer(1), x_peer(2), x_peer(3), z_peer, next_dev, prev_dev):
        pl.semaphore_signal(barrier, inc=1, device_id=target, device_id_type=MESH)
    pl.semaphore_wait(barrier, 7)

    def w_send(i):
        block = w16.at[i, pl.ds(mine, T)]
        return remote(block, block, w_ssem.at[i], w_rsem.at[i], partner)

    def m_remote(i):
        return remote(m_send.at[i], m_recv.at[i], m_ssem.at[i], m_rsem.at[i], partner)

    def halo_copy(which, c):
        source = (k_in, v_in)[which]
        return remote(
            source.at[c], halo.at[which, c], h_ssem.at[which, c], h_rsem.at[which, c], next_dev
        )

    @pl.loop(0, 6)
    def _(i):
        w_copy(i).wait()
        w16[i, pl.ds(mine, T)] = w32[i, pl.ds(mine, T)].astype(BF16)
        w_send(i).start()

    halo_copy(0, 0).start()
    halo_copy(1, 0).start()
    k_copy.wait()
    v_copy.wait()

    @pl.loop(0, 6)
    def _(i):
        m_copy(i).wait()
        m_send[i] = m32[i, pl.ds(mine, T)].astype(BF16)
        m_remote(i).start()

    q_copy.wait()

    def split(u):
        c = lax.div(u, 6)
        m = lax.rem(u, 6)
        h = lax.div(m, 3)
        jj = lax.rem(m, 3)
        return c, h, jj, h * 3 + lax.rem(jj + 2, 3), m

    row_id = lax.broadcasted_iota(jnp.int32, (T, T), 0)
    col_id = lax.broadcasted_iota(jnp.int32, (T, T), 1)

    def keys(u):
        c, h, _, _, _ = split(u)

        @pl.when(c == 0)
        def _():
            for j in range(3):
                w_send(h * 3 + j).wait_recv()

        base = c * 6 + h * 3
        lanes = pl.ds(pl.multiple_of(h * DH, DH), DH)
        unit = unit_rows(kv[c, :, lanes])
        left[1] = unit
        gate = dot(unit, w16[base])
        up = dot(unit, w16[base + 1])
        sig = jax.nn.sigmoid(gate)
        silu = gate * sig
        left[0] = (silu * up).astype(BF16)
        lr = lr_in[h, pl.ds(c, 1), :]
        lr = jnp.sum(jnp.where(row_id == col_id, lr, 0.0), axis=1, keepdims=True)
        target = (-(lr * vv[c, :, lanes].astype(F32))).astype(BF16)
        right[0] = target
        back = dot(target, w16[base + 2], ((1,), (1,)))
        right[1] = (back * up * sig * (1.0 + gate * (1.0 - sig))).astype(BF16)
        right[2] = (back * silu).astype(BF16)

    def a_copy(u):
        m = lax.rem(u, 6)
        return remote(send_a.at[m], recv_a.at[u], ssem.at[0, u], rsem.at[0, u], partner)

    def stage_a(u):
        @pl.when(lax.rem(u, 3) == 0)
        def _():
            keys(u)

        _, _, jj, _, m = split(u)
        li = jnp.minimum(jj, 1)
        rhs = right[jj]
        send_a[m] = dot(left[li, :, pl.ds(theirs, T)], rhs, ((0,), (0,))).astype(BF16)
        a_copy(u).start()
        own[m] = dot(left[li, :, pl.ds(mine, T)], rhs, ((0,), (0,)))

    def by_type(u, fn):
        even = lax.rem(u, 2) == 0

        @pl.when(even)
        def _():
            fn(True)

        @pl.when(jnp.logical_not(even))
        def _():
            fn(False)

    def wait_rows(stage, u, rows, send):
        block = total.at[u, pl.ds(0, rows)]
        copy = remote(block, block, ssem.at[stage, u], rsem.at[stage, u], partner)
        if send:
            copy.wait_send()
        else:
            copy.wait_recv()

    def stage_b1(u):
        m = lax.rem(u, 6)
        a_copy(u).wait_recv()
        summed = own[m] + recv_a[u].astype(F32)
        own[m] = summed
        send_b[m] = summed.astype(BF16)

        def go(z_first):
            if z_first:
                remote(
                    send_b.at[m, pl.ds(pl.multiple_of((1 - z) * 128, 128), 128)],
                    recv_b1.at[u, pl.ds(0, 128)], ssem.at[1, u], rsem.at[1, u], z_peer,
                ).start()
            else:
                for k in (2, 1, 3):
                    remote(
                        send_b.at[m, pl.ds(pl.multiple_of(x_of(k) * 64, 64), 64)],
                        recv_b1.at[u, pl.ds((k - 1) * 64, 64)],
                        ssem.at[1, u], rsem.at[1, u], x_peer(k),
                    ).start()

        by_type(u, go)

    def stage_b2(u):
        m = lax.rem(u, 6)

        def go(z_first):
            if z_first:
                wait_rows(1, u, 128, False)
                keep = pl.ds(pl.multiple_of(z * 128, 128), 128)
                summed = own[m, keep] + recv_b1[u, pl.ds(0, 128)].astype(F32)
                own[m, keep] = summed
                send_b2[m] = summed.astype(BF16)
                for k in (2, 1, 3):
                    remote(
                        send_b2.at[m, pl.ds(pl.multiple_of(x_of(k) * 32, 32), 32)],
                        recv_b2.at[u, pl.ds((k - 1) * 32, 32)],
                        ssem.at[2, u], rsem.at[2, u], x_peer(k),
                    ).start()
            else:
                wait_rows(1, u, 192, False)
                keep = pl.ds(pl.multiple_of(x * 64, 64), 64)
                summed = own[m, keep]
                for k in range(3):
                    summed = summed + recv_b1[u, pl.ds(k * 64, 64)].astype(F32)
                own[m, keep] = summed
                send_b2[m, pl.ds(0, 64)] = summed.astype(BF16)
                remote(
                    send_b2.at[m, pl.ds(pl.multiple_of((1 - z) * 32, 32), 32)],
                    recv_b2.at[u, pl.ds(0, 32)], ssem.at[2, u], rsem.at[2, u], z_peer,
                ).start()

        by_type(u, go)

    def stage_c1(u):
        m = lax.rem(u, 6)

        def go(z_first):
            if z_first:
                wait_rows(2, u, 96, False)
                at = z * 128 + x * 32
                count = 3
            else:
                wait_rows(2, u, 32, False)
                at = x * 64 + z * 32
                count = 1
            at = pl.multiple_of(at, 32)
            summed = own[m, pl.ds(at, 32)]
            for k in range(count):
                summed = summed + recv_b2[u, pl.ds(k * 32, 32)].astype(F32)
            place = pl.ds(pl.multiple_of(row * T + at, 32), 32)
            total[u, place] = summed.astype(BF16)
            block = total.at[u, place]
            if z_first:
                for k in (2, 1, 3):
                    remote(block, block, ssem.at[3, u], rsem.at[3, u], x_peer(k)).start()
            else:
                remote(block, block, ssem.at[3, u], rsem.at[3, u], z_peer).start()

        by_type(u, go)

    def stage_c2(u):
        def go(z_first):
            if z_first:
                wait_rows(3, u, 96, False)
                place = pl.ds(pl.multiple_of(row * T + z * 128, 128), 128)
                block = total.at[u, place]
                remote(block, block, ssem.at[4, u], rsem.at[4, u], z_peer).start()
            else:
                wait_rows(3, u, 32, False)
                place = pl.ds(pl.multiple_of(row * T + x * 64, 64), 64)
                block = total.at[u, place]
                for k in (2, 1, 3):
                    remote(block, block, ssem.at[4, u], rsem.at[4, u], x_peer(k)).start()

        by_type(u, go)

    def stage_d(u):
        by_type(u, lambda z_first: wait_rows(4, u, 128 if z_first else 192, False))
        block = total.at[u, pl.ds(mine, T)]
        remote(block, block, ssem.at[5, u], rsem.at[5, u], partner).start()

    def out_copies(i):
        h, j = lax.div(i, 3), lax.rem(i, 3)
        return (
            pltpu.make_async_copy(w32.at[i, pl.ds(mine, T)], w_out.at[h, j], out_sem.at[0, i]),
            pltpu.make_async_copy(m32.at[i, pl.ds(mine, T)], m_out.at[h, j], out_sem.at[1, i]),
        )

    def stage_n(u):
        c, h, _, i, m = split(u)
        wait_rows(5, u, T, False)

        @pl.when(c == 0)
        def _():
            m_remote(i).wait_recv()
            m32[i, pl.ds(theirs, T)] = m_recv[i].astype(F32)
            w32[i, pl.ds(theirs, T)] = w16[i, pl.ds(theirs, T)].astype(F32)

        rate = rate_in[h]
        squares = jnp.zeros((1, DH), F32)
        for b in range(4):
            rows = pl.ds(b * 128, 128)
            moment = rate * m32[i, rows] + total[u, rows].astype(F32)
            m32[i, rows] = moment
            squares = squares + jnp.sum(moment * moment, axis=0, keepdims=True)
        inverse = lax.rsqrt(jnp.sum(squares, axis=1, keepdims=True) + 1e-06)
        for b in range(4):
            rows = pl.ds(b * 128, 128)
            ortho[rows] = (m32[i, rows] * inverse).astype(BF16)
        for _ in range(2):
            for b in range(4):
                rows = pl.ds(b * 128, 128)
                part = dot(ortho[:, rows], ortho[...], ((0,), (0,)))
                gram[rows] = part
                gram16[rows] = part.astype(BF16)
            for b in range(4):
                rows = pl.ds(b * 128, 128)
                square = dot(gram16[rows], gram16[...])
                poly[rows] = (QUINTIC[1] * gram[rows] + QUINTIC[2] * square).astype(BF16)
            for b in range(4):
                rows = pl.ds(b * 128, 128)
                old = ortho[rows]
                turned = dot(old, poly[...])
                ortho[rows] = (QUINTIC[0] * old.astype(F32) + turned).astype(BF16)
        step = step_in[h]
        columns = jnp.zeros((1, DH), F32)
        for b in range(4):
            rows = pl.ds(b * 128, 128)
            stepped = w32[i, rows] - step * ortho[rows].astype(F32)
            w32[i, rows] = stepped
            columns = columns + jnp.sum(stepped * stepped, axis=0, keepdims=True)
        scale = lax.rsqrt(columns + 1e-06)
        for b in range(4):
            rows = pl.ds(b * 128, 128)
            w32[i, rows] = w32[i, rows] * scale

        @pl.when(c == 0)
        def _():
            for b in range(4):
                rows = pl.ds(b * 128, 128)
                w16[6 + i, rows] = w32[i, rows].astype(BF16)

        @pl.when(c == 1)
        def _():
            for copy in out_copies(i):
                copy.start()

        wait_rows(0, u, T, True)
        by_type(u, lambda z_first: wait_rows(1, u, 128 if z_first else 192, True))
        by_type(u, lambda z_first: wait_rows(2, u, 96 if z_first else 32, True))
        by_type(u, lambda z_first: wait_rows(3, u, 96 if z_first else 32, True))
        by_type(u, lambda z_first: wait_rows(4, u, 128 if z_first else 192, True))
        wait_rows(5, u, T, True)

    first = device == 0
    near = col_id <= row_id

    def mix_copy(c, h):
        lanes = pl.ds(pl.multiple_of(h * DH, DH), DH)
        return pltpu.make_async_copy(
            mix.at[c, :, lanes], mixed_out.at[c, :, lanes], mix_sem.at[c, h]
        )

    def fill(c, h):
        base = c * 6 + h * 3
        lanes = pl.ds(pl.multiple_of(h * DH, DH), DH)
        unit = unit_rows(qv[c, :, lanes])
        gate = dot(unit, w16[base])
        up = dot(unit, w16[base + 1])
        hidden = (gate * jax.nn.sigmoid(gate) * up).astype(BF16)
        recall[...] = dot(hidden, w16[base + 2])

        @pl.when(h == 0)
        def _():
            halo_copy(0, c).wait_recv()
            halo_copy(1, c).wait_recv()

        hc = jnp.maximum(c - first.astype(jnp.int32), 0)
        bias = jnp.where(jnp.logical_and(first, c == 0), -1e30, 0.0)
        for a in range(4):
            part = pl.ds(pl.multiple_of(h * DH + a * HEAD_DIM, HEAD_DIM), HEAD_DIM)
            query = qv[c, :, part]
            here = dot(query, kv[c, :, part], ((1,), (1,)))
            there = dot(query, halo[0, hc, :, part], ((1,), (1,)))
            scale = HEAD_DIM ** (-0.5)
            scores = jnp.where(near, here * scale, there * scale + bias)
            top = jnp.max(scores, axis=-1, keepdims=True)
            expo = jnp.exp(scores - top)
            probs = expo / jnp.sum(expo, axis=-1, keepdims=True)
            near_probs = jnp.where(near, probs, 0.0).astype(BF16)
            far_probs = jnp.where(near, 0.0, probs).astype(BF16)
            result = dot(near_probs, vv[c, :, part]) + dot(far_probs, halo[1, hc, :, part])
            local = pl.ds(a * HEAD_DIM, HEAD_DIM)
            mix[c, :, part] = (recall[:, local] + result).astype(BF16)
        mix_copy(c, h).start()

    @pl.loop(0, 21)
    def _(i):
        def at(lag, fn):
            slot = i - lag
            early = jnp.logical_and(slot >= 0, slot < 6)
            late = jnp.logical_and(slot >= 9, slot < 15)
            u = jnp.where(slot >= 9, slot - 3, slot)

            @pl.when(jnp.logical_or(early, late))
            def _():
                fn(u)

        at(0, stage_a)
        at(5, stage_d)
        at(4, stage_c2)
        at(3, stage_c1)
        at(2, stage_b2)
        at(1, stage_b1)

        @pl.when(i == 7)
        def _():
            halo_copy(0, 1).start()
            halo_copy(1, 1).start()

        fills = jnp.logical_or(
            jnp.logical_or(i == 6, i == 7), jnp.logical_or(i == 15, i == 16)
        )

        @pl.when(fills)
        def _():
            c = jnp.where(i >= 15, 1, 0)
            fill(c, i - jnp.where(i >= 15, 15, 6))

        at(6, stage_n)

    @pl.loop(0, 6)
    def _(i):
        w_send(i).wait_send()
        m_remote(i).wait_send()
        for copy in out_copies(i):
            copy.wait()

    for c in range(2):
        halo_copy(0, c).wait_send()
        halo_copy(1, c).wait_send()
        for h in range(2):
            mix_copy(c, h).wait()


def shards(queries, keys, values, token_lr, momentum_rate, update_step, fast_weights, momentum):
    hbm = pl.BlockSpec(memory_space=pl.ANY)
    vmem = pl.BlockSpec(memory_space=pltpu.VMEM)
    smem = pl.BlockSpec(memory_space=pltpu.SMEM)
    dma = pltpu.SemaphoreType.DMA
    return pl.pallas_call(
        kernel,
        out_shape=(
            jax.ShapeDtypeStruct(queries.shape, BF16),
            jax.ShapeDtypeStruct(fast_weights.shape, F32),
            jax.ShapeDtypeStruct(momentum.shape, F32),
        ),
        in_specs=[hbm, hbm, hbm, vmem, smem, smem, hbm, hbm],
        out_specs=(hbm, hbm, hbm),
        scratch_shapes=[
            pltpu.VMEM((2, T, 1024), BF16),
            pltpu.VMEM((2, T, 1024), BF16),
            pltpu.VMEM((2, T, 1024), BF16),
            pltpu.VMEM((2, 2, T, 1024), BF16),
            pltpu.VMEM((2, T, 1024), BF16),
            pltpu.VMEM((T, DH), F32),
            pltpu.VMEM((6, DH, DH), F32),
            pltpu.VMEM((6, DH, DH), F32),
            pltpu.VMEM((12, DH, DH), BF16),
            pltpu.VMEM((6, T, DH), BF16),
            pltpu.VMEM((6, T, DH), BF16),
            pltpu.VMEM((2, T, DH), BF16),
            pltpu.VMEM((3, T, DH), BF16),
            pltpu.VMEM((6, T, DH), BF16),
            pltpu.VMEM((UNITS, T, DH), BF16),
            pltpu.VMEM((6, T, DH), F32),
            pltpu.VMEM((6, T, DH), BF16),
            pltpu.VMEM((UNITS, 192, DH), BF16),
            pltpu.VMEM((6, 128, DH), BF16),
            pltpu.VMEM((UNITS, 96, DH), BF16),
            pltpu.VMEM((UNITS, DH, DH), BF16),
            pltpu.VMEM((DH, DH), BF16),
            pltpu.VMEM((DH, DH), F32),
            pltpu.VMEM((DH, DH), BF16),
            pltpu.VMEM((DH, DH), BF16),
            dma((3,)), dma((6,)), dma((6,)), dma((6,)), dma((6,)), dma((6,)), dma((6,)),
            dma((2, 2)), dma((2, 2)),
            dma((6, UNITS)), dma((6, UNITS)), dma((2, 6)), dma((2, 2)),
        ],
        compiler_params=pltpu.CompilerParams(
            collective_id=0, has_side_effects=True, vmem_limit_bytes=66_000_000
        ),
    )(queries, keys, values, token_lr, momentum_rate, update_step, fast_weights, momentum)


def solution(mesh):
    wide = P(None, ("tok", "row"), "mem")
    state = P("mem", None, "row", None)
    return jax.shard_map(
        shards,
        mesh=mesh,
        in_specs=(wide, wide, wide, P("mem", None, ("tok", "row")), P("mem"), P("mem"), state, state),
        out_specs=(wide, state, state),
        check_vma=False,
    )
```

time: 446 us -> 138 us (0.31); the launches traced: 440 us -> 137 us
  waiting for transfers between devices: 263 us -> 0 us
  Pallas kernels: 0 us -> 128 us
  matrix products: 64.1 us -> 0 us
  other arithmetic: 52 us -> 0 us
  local copies, waits for them, and re-layouts: 36.3 us -> 8.21 us
  between operations: 14.7 us -> 0.64 us
  blocking collectives: 7.62 us -> 0 us
    psum x2 -> x0, waiting for transfers between devices: 229 us -> none  [shards(): lax.psum(gradient.astype(jnp.bfloat16), ('tok', 'row')).astype(jnp.float32)]
    pallas_call x0 -> x1, Pallas kernels: none -> 128 us  [shards(): pl.pallas_call(kernel, out_shape=(jax.ShapeDtypeStruct(queries.shape, BF1...]
    dot_general x30 -> x0, matrix products: 64.1 us -> none  [the longest x4 9.87 us: refine(): jnp.einsum('hmde,hmef->hmdf', gram_half, gram_half, preferred_element_typ...]
    all_gather x4 -> x0, waiting for transfers between devices: 33.9 us -> none  [the longest x2 17.5 us: shards(): lax.all_gather(weights.astype(jnp.bfloat16), 'row', axis=2, tiled=True)]
    convert_element_type x7 -> x0, other arithmetic: 19.9 us -> none  [the longest x2 9.06 us: shards(): moment.astype(jnp.bfloat16)]
    reduce_sum x6 -> x0, other arithmetic: 11.1 us -> none  [the longest x2 5.71 us: shards(): jnp.sum(whole * whole, axis=(2, 3), keepdims=True) + 1e-06]
    sub x1 -> x0, other arithmetic: 9.43 us -> none  [attend(): expo = jnp.exp(scores - top)]
    convert_element_type x4 -> x0, local copies, waits for them, and re-layouts: 9.34 us -> none  [the longest x2 6.23 us: shards(): value_heads[index].astype(jnp.float32)]
  transfers between devices with their start and end apart: 7 -> 0, of which waited for: 5 -> 0; matrix products, arithmetic and copies ran while one was open for 20% -> 0% of each run, Pallas kernels for 0% -> 0%
where the time goes in v1:
time: 138 us; the launch traced here: 137 us
  Pallas kernels  128 us (93%)
  local copies, waits for them, and re-layouts  8.21 us (6%)
    pallas_call x1, Pallas kernels, shards(): pl.pallas_call(kernel, out_shape=(jax.ShapeDtypeStruct(queries.shape, BF1...  128 us
    unnamed x5, local copies, waits for them, and re-layouts  8.21 us

profile of v1, /device:TPU:1, one launch (start us, length us, event | category | flops | bytes accessed | tf_op | source)
XLA Modules:
  0.0 136.8 jit_solution(15609754174521639247)
XLA Ops:
  0.6 128.0 %shard_map.103 = (bf16[2,256,1024]{2,1,0:T(8,128)(2,1)}, f32[2,3,256,512]{3,2,1,0:T(8,128)}, f32[2,3,256,512]{3,2,1,0:T(8,128)}) custom-call(bf16[2,256,1024]{2,1,0:T(8,128)(2,1)} %q_in.1, bf16[2,256,1024]{2,1,0:T(8,128)(2,1)} %k_in.1, bf16[2,256,1024]{2,1,0:T(8,128)(2,1)} %v_in.1, f32[2,2,256]{2,1,0:T(2,128)} %lr_in.1, f32[2]{0:T(128)} %rate_in.1, ...), custom_call_target="tpu_custom_call" | custom-call | tf_op jit(solution)/shard_map/pallas_call | solution.py:473
  128.6 2.3 %copy.14 = bf16[2,256,1024]{2,1,0:T(8,128)(2,1)} copy(bf16[2,256,1024]{2,1,0:T(8,128)(2,1)} %get-tuple-element.6) | data formatting | bytes 2097152
  130.9 0.0 copy-start
  130.9 4.3 %copy.15 = f32[2,3,256,512]{3,2,1,0:T(8,128)} copy(f32[2,3,256,512]{3,2,1,0:T(8,128)} %get-tuple-element.7) | data formatting | bytes 6291456
  135.2 0.0 copy-done
  135.2 1.7 %copy.16 = f32[2,3,256,512]{3,2,1,0:T(8,128)} copy(f32[2,3,256,512]{3,2,1,0:T(8,128)S(1)} %copy-done) | data formatting | bytes 6291456
Async XLA Ops:
  130.9 4.3 %copy-start = (f32[2,3,256,512]{3,2,1,0:T(8,128)S(1)}, f32[2,3,256,512]{3,2,1,0:T(8,128)}, u32[]{:S(2)}) copy-start(f32[2,3,256,512]{3,2,1,0:T(8,128)} %get-tuple-element.8) | copy-start | bytes 9437188

commit v2 on v1

v2 whole, which is shorter than its diff:
```python
import jax
import jax.numpy as jnp
from jax import lax
from jax.experimental import pallas as pl
from jax.experimental.pallas import tpu as pltpu
from jax.sharding import PartitionSpec as P

DH = 512
HEAD_DIM = 128
QUINTIC = (3.4445, -4.775, 2.0315)
MESH = pl.DeviceIdType.MESH
F32 = jnp.float32
BF16 = jnp.bfloat16
T = 256
UNITS = 12
ZC, XC = 384, 128
ROWS_1 = (128 * ZC + 192 * XC) // DH
ROWS_2 = (96 * ZC + 32 * XC) // DH

STEPS = 59
PLAN = (
    ("H", (16777217, 0,)),
    ("A", (805306927, 226,)),
    ("B1", (4217, 1811,)),
    ("B2", (69056, 23200,)),
    ("F", (36864, 5120,)),
    ("C2", (10919936, 710656,)),
    ("D", (107282432, 6660096,)),
    ("C1", (619008, 56832,)),
    ("NA", (563347456, 14237697,)),
    ("NB", (581435392, 15368193,)),
    ("E", (234881024, 528482318,)),
)


def dot(a, b, dims=((1,), (0,))):
    return lax.dot_general(a, b, (dims, ((), ())), preferred_element_type=F32)


def unit_rows(field):
    field = field.astype(F32)
    return (field * lax.rsqrt(jnp.mean(field * field, axis=-1, keepdims=True) + 1e-05)).astype(BF16)


def kernel(
    q_in, k_in, v_in, lr_in, rate_in, step_in, w_in, m_in,
    mixed_out, w_out, m_out,
    qv, kv, vv, halo, mix, recall, w32, m32, w16, m_send, m_recv,
    left, right, send_a, recv_a, own, send_b, recv_b1, send_b2, recv_b2, total,
    ortho, gram, gram16, poly, x_send, x_recv, s_send, s_recv,
    load_sem, w_load, m_load, w_ssem, w_rsem, m_ssem, m_rsem, h_ssem, h_rsem,
    ssem, rsem, out_sem, mix_sem,
):
    tok = lax.axis_index("tok")
    row = lax.axis_index("row")
    x = lax.rem(tok, 4)
    z = lax.div(tok, 4)
    other = 1 - row
    z_tok = lax.rem(tok + 4, 8)
    device = tok * 2 + row
    after = lax.rem(device + 1, 16)
    before = lax.rem(device + 15, 16)
    mine = pl.multiple_of(row * T, T)
    theirs = pl.multiple_of(other * T, T)

    def chip(t):
        return {"tok": t, "row": row}

    partner = {"tok": tok, "row": other}
    z_peer = chip(z_tok)
    next_dev = {"tok": lax.div(after, 2), "row": lax.rem(after, 2)}
    prev_dev = {"tok": lax.div(before, 2), "row": lax.rem(before, 2)}

    def x_of(k):
        return lax.rem(x + k, 4)

    def x_peer(k):
        return chip(z * 4 + x_of(k))

    def remote(src, dst, send, recv, target):
        return pltpu.make_async_remote_copy(
            src_ref=src, dst_ref=dst, send_sem=send, recv_sem=recv,
            device_id=target, device_id_type=MESH,
        )

    def w_copy(i):
        return pltpu.make_async_copy(
            w_in.at[lax.div(i, 3), lax.rem(i, 3)], w32.at[i, pl.ds(mine, T)], w_load.at[i]
        )

    def m_copy(i):
        return pltpu.make_async_copy(
            m_in.at[lax.div(i, 3), lax.rem(i, 3)], m32.at[i, pl.ds(mine, T)], m_load.at[i]
        )

    k_copy = pltpu.make_async_copy(k_in, kv, load_sem.at[0])
    v_copy = pltpu.make_async_copy(v_in, vv, load_sem.at[1])
    q_copy = pltpu.make_async_copy(q_in, qv, load_sem.at[2])

    @pl.loop(0, 6)
    def _(i):
        w_copy(i).start()

    k_copy.start()
    v_copy.start()

    @pl.loop(0, 6)
    def _(i):
        m_copy(i).start()

    q_copy.start()

    barrier = pltpu.get_barrier_semaphore()
    for target in (partner, x_peer(1), x_peer(2), x_peer(3), z_peer, next_dev, prev_dev):
        pl.semaphore_signal(barrier, inc=1, device_id=target, device_id_type=MESH)
    pl.semaphore_wait(barrier, 7)

    def w_send(i):
        block = w16.at[i, pl.ds(mine, T)]
        return remote(block, block, w_ssem.at[i], w_rsem.at[i], partner)

    def m_remote(t):
        return remote(m_send.at[t], m_recv.at[t], m_ssem.at[t], m_rsem.at[t], partner)

    def matrix(m):
        return lax.div(m, 3) * 3 + lax.rem(lax.rem(m, 3) + 2, 3)

    def halo_copy(which, c):
        source = (k_in, v_in)[which]
        return remote(
            source.at[c], halo.at[which, c], h_ssem.at[which, c], h_rsem.at[which, c], next_dev
        )

    @pl.loop(0, 6)
    def _(i):
        w_copy(i).wait()
        w16[i, pl.ds(mine, T)] = w32[i, pl.ds(mine, T)].astype(BF16)
        w_send(i).start()

    k_copy.wait()
    v_copy.wait()

    @pl.loop(0, 6)
    def _(i):
        m_copy(i).wait()

    @pl.loop(0, 3)
    def _(t):
        m_send[t] = m32[matrix(2 * t + other), pl.ds(mine, T)].astype(BF16)
        m_remote(t).start()

    q_copy.wait()

    def split(u):
        c = lax.div(u, 6)
        m = lax.rem(u, 6)
        h = lax.div(m, 3)
        jj = lax.rem(m, 3)
        return c, h, jj, matrix(m), m

    row_id = lax.broadcasted_iota(jnp.int32, (T, T), 0)
    col_id = lax.broadcasted_iota(jnp.int32, (T, T), 1)

    def keys(u):
        c, h, _, _, _ = split(u)

        @pl.when(c == 0)
        def _():
            for j in range(3):
                w_send(h * 3 + j).wait_recv()

        base = c * 6 + h * 3
        lanes = pl.ds(pl.multiple_of(h * DH, DH), DH)
        unit = unit_rows(kv[c, :, lanes])
        left[1] = unit
        gate = dot(unit, w16[base])
        up = dot(unit, w16[base + 1])
        sig = jax.nn.sigmoid(gate)
        silu = gate * sig
        left[0] = (silu * up).astype(BF16)
        lr = lr_in[h, pl.ds(c, 1), :]
        lr = jnp.sum(jnp.where(row_id == col_id, lr, 0.0), axis=1, keepdims=True)
        target = (-(lr * vv[c, :, lanes].astype(F32))).astype(BF16)
        right[0] = target
        back = dot(target, w16[base + 2], ((1,), (1,)))
        right[1] = (back * up * sig * (1.0 + gate * (1.0 - sig))).astype(BF16)
        right[2] = (back * silu).astype(BF16)

    def a_copy(u):
        m = lax.rem(u, 6)
        return remote(send_a.at[m], recv_a.at[u], ssem.at[0, u], rsem.at[0, u], partner)

    def stage_a(u):
        @pl.when(lax.rem(u, 3) == 0)
        def _():
            keys(u)

        _, _, jj, _, m = split(u)
        li = jnp.minimum(jj, 1)
        rhs = right[jj]
        send_a[m] = dot(left[li, :, pl.ds(theirs, T)], rhs, ((0,), (0,))).astype(BF16)
        a_copy(u).start()
        own[m] = dot(left[li, :, pl.ds(mine, T)], rhs, ((0,), (0,)))

    def wait_rows(stage, u, rows, send):
        block = total.at[u, pl.ds(0, rows)]
        copy = remote(block, block, ssem.at[stage, u], rsem.at[stage, u], partner)
        if send:
            copy.wait_send()
        else:
            copy.wait_recv()

    z_cols, x_cols = pl.ds(0, ZC), pl.ds(ZC, XC)

    def stage_b1(u):
        m = lax.rem(u, 6)
        a_copy(u).wait_recv()
        summed = own[m] + recv_a[u].astype(F32)
        own[m] = summed
        send_b[m] = summed.astype(BF16)

        remote(
            send_b.at[m, pl.ds(pl.multiple_of((1 - z) * 128, 128), 128), z_cols],
            recv_b1.at[u, pl.ds(0, 128), z_cols], ssem.at[1, u], rsem.at[1, u], z_peer,
        ).start()
        for k in (2, 1, 3):
            remote(
                send_b.at[m, pl.ds(pl.multiple_of(x_of(k) * 64, 64), 64), x_cols],
                recv_b1.at[u, pl.ds((k - 1) * 64, 64), x_cols],
                ssem.at[1, u], rsem.at[1, u], x_peer(k),
            ).start()

    def stage_b2(u):
        m = lax.rem(u, 6)
        wait_rows(1, u, ROWS_1, False)
        keep = pl.ds(pl.multiple_of(z * 128, 128), 128)
        summed = own[m, keep, z_cols] + recv_b1[u, pl.ds(0, 128), z_cols].astype(F32)
        own[m, keep, z_cols] = summed
        send_b2[m, :, z_cols] = summed.astype(BF16)
        for k in (2, 1, 3):
            remote(
                send_b2.at[m, pl.ds(pl.multiple_of(x_of(k) * 32, 32), 32), z_cols],
                recv_b2.at[u, pl.ds((k - 1) * 32, 32), z_cols],
                ssem.at[2, u], rsem.at[2, u], x_peer(k),
            ).start()
        keep = pl.ds(pl.multiple_of(x * 64, 64), 64)
        summed = own[m, keep, x_cols]
        for k in range(3):
            summed = summed + recv_b1[u, pl.ds(k * 64, 64), x_cols].astype(F32)
        own[m, keep, x_cols] = summed
        send_b2[m, pl.ds(0, 64), x_cols] = summed.astype(BF16)
        remote(
            send_b2.at[m, pl.ds(pl.multiple_of((1 - z) * 32, 32), 32), x_cols],
            recv_b2.at[u, pl.ds(0, 32), x_cols], ssem.at[2, u], rsem.at[2, u], z_peer,
        ).start()

    def stage_c1(u):
        m = lax.rem(u, 6)
        wait_rows(2, u, ROWS_2, False)
        for place, cols, count in ((z * 128 + x * 32, z_cols, 3), (x * 64 + z * 32, x_cols, 1)):
            summed = own[m, pl.ds(pl.multiple_of(place, 32), 32), cols]
            for k in range(count):
                summed = summed + recv_b2[u, pl.ds(k * 32, 32), cols].astype(F32)
            at = pl.ds(pl.multiple_of(row * T + place, 32), 32)
            total[u, at, cols] = summed.astype(BF16)
            block = total.at[u, at, cols]
            for target in (x_peer(2), x_peer(1), x_peer(3)) if count == 3 else (z_peer,):
                remote(block, block, ssem.at[3, u], rsem.at[3, u], target).start()

    def stage_c2(u):
        wait_rows(3, u, ROWS_2, False)
        block = total.at[u, pl.ds(pl.multiple_of(row * T + z * 128, 128), 128), z_cols]
        remote(block, block, ssem.at[4, u], rsem.at[4, u], z_peer).start()
        block = total.at[u, pl.ds(pl.multiple_of(row * T + x * 64, 64), 64), x_cols]
        for k in (2, 1, 3):
            remote(block, block, ssem.at[4, u], rsem.at[4, u], x_peer(k)).start()

    def handles(u):
        return lax.rem(u, 2) == row

    def d_copy(u):
        block = total.at[u, pl.ds(mine, T)]
        return remote(block, block, ssem.at[5, u], rsem.at[5, u], partner)

    def stage_d(u):
        wait_rows(4, u, ROWS_1, False)

        @pl.when(jnp.logical_not(handles(u)))
        def _():
            d_copy(u).start()

    def out_copies(i):
        h, j = lax.div(i, 3), lax.rem(i, 3)
        return (
            pltpu.make_async_copy(w32.at[i, pl.ds(mine, T)], w_out.at[h, j], out_sem.at[0, i]),
            pltpu.make_async_copy(m32.at[i, pl.ds(mine, T)], m_out.at[h, j], out_sem.at[1, i]),
        )

    def newton_schulz():
        for b in range(4):
            rows = pl.ds(b * 128, 128)
            part = dot(ortho[:, rows], ortho[...], ((0,), (0,)))
            gram[rows] = part
            gram16[rows] = part.astype(BF16)
        for b in range(4):
            rows = pl.ds(b * 128, 128)
            square = dot(gram16[rows], gram16[...])
            poly[rows] = (QUINTIC[1] * gram[rows] + QUINTIC[2] * square).astype(BF16)
        for b in range(4):
            rows = pl.ds(b * 128, 128)
            old = ortho[rows]
            turned = dot(old, poly[...])
            ortho[rows] = (QUINTIC[0] * old.astype(F32) + turned).astype(BF16)

    def stage_na(u):
        c, h, _, i, m = split(u)
        rate = rate_in[h]

        @pl.when(handles(u))
        def _():
            wait_rows(5, u, T, False)

            @pl.when(c == 0)
            def _():
                t = lax.div(m, 2)
                m_remote(t).wait_recv()
                m32[i, pl.ds(theirs, T)] = m_recv[t].astype(F32)

            squares = jnp.zeros((1, DH), F32)
            for b in range(4):
                rows = pl.ds(b * 128, 128)
                moment = rate * m32[i, rows] + total[u, rows].astype(F32)
                m32[i, rows] = moment
                squares = squares + jnp.sum(moment * moment, axis=0, keepdims=True)
            inverse = lax.rsqrt(jnp.sum(squares, axis=1, keepdims=True) + 1e-06)
            for b in range(4):
                rows = pl.ds(b * 128, 128)
                ortho[rows] = (m32[i, rows] * inverse).astype(BF16)
            newton_schulz()

        @pl.when(jnp.logical_not(handles(u)))
        def _():
            rows = pl.ds(mine, T)
            m32[i, rows] = rate * m32[i, rows] + total[u, rows].astype(F32)

    def x_copy(u):
        return remote(
            x_send.at[lax.rem(u, 6)], x_recv.at[u], ssem.at[6, u], rsem.at[6, u], partner
        )

    def s_copy(u):
        return remote(
            s_send.at[lax.rem(u, 6)], s_recv.at[u], ssem.at[7, u], rsem.at[7, u], partner
        )

    def half_copy(u, i, start):
        block = w16.at[6 + i, pl.ds(start, T)]
        return remote(block, block, ssem.at[8, u], rsem.at[8, u], partner)

    def stage_nb(u):
        c, h, _, i, m = split(u)

        @pl.when(handles(u))
        def _():
            @pl.when(c == 0)
            def _():
                w32[i, pl.ds(theirs, T)] = w16[i, pl.ds(theirs, T)].astype(F32)

            newton_schulz()
            x_send[m] = ortho[pl.ds(theirs, T)]
            x_copy(u).start()
            step = step_in[h]
            columns = jnp.zeros((1, DH), F32)
            for b in range(4):
                rows = pl.ds(b * 128, 128)
                stepped = w32[i, rows] - step * ortho[rows].astype(F32)
                w32[i, rows] = stepped
                columns = columns + jnp.sum(stepped * stepped, axis=0, keepdims=True)
            scale = lax.rsqrt(columns + 1e-06)
            s_send[m] = jnp.broadcast_to(scale, (8, DH))
            s_copy(u).start()

            @pl.when(c == 0)
            def _():
                for start in (mine, theirs):
                    for b in range(2):
                        rows = pl.ds(pl.multiple_of(start + b * 128, 128), 128)
                        scaled = w32[i, rows] * scale
                        w32[i, rows] = scaled
                        w16[6 + i, rows] = scaled.astype(BF16)
                    if start is mine:
                        half_copy(u, i, mine).start()

            @pl.when(c == 1)
            def _():
                rows = pl.ds(mine, T)
                w32[i, rows] = w32[i, rows] * scale
                for copy in out_copies(i):
                    copy.start()

    def stage_e(u):
        c, h, _, i, m = split(u)

        @pl.when(jnp.logical_not(handles(u)))
        def _():
            x_copy(u).wait_recv()
            s_copy(u).wait_recv()
            rows = pl.ds(mine, T)
            scale = s_recv[u, pl.ds(0, 1), :]
            scaled = (w32[i, rows] - step_in[h] * x_recv[u].astype(F32)) * scale
            w32[i, rows] = scaled

            @pl.when(c == 0)
            def _():
                w16[6 + i, rows] = scaled.astype(BF16)
                half_copy(u, i, theirs).wait_recv()

            @pl.when(c == 1)
            def _():
                for copy in out_copies(i):
                    copy.start()

            d_copy(u).wait_send()

        @pl.when(handles(u))
        def _():
            x_copy(u).wait_send()
            s_copy(u).wait_send()

            @pl.when(c == 0)
            def _():
                half_copy(u, i, mine).wait_send()

        wait_rows(0, u, T, True)
        wait_rows(1, u, ROWS_1, True)
        wait_rows(2, u, ROWS_2, True)
        wait_rows(3, u, ROWS_2, True)
        wait_rows(4, u, ROWS_1, True)

    first = device == 0
    near = col_id <= row_id

    def mix_copy(c, h):
        lanes = pl.ds(pl.multiple_of(h * DH, DH), DH)
        return pltpu.make_async_copy(
            mix.at[c, :, lanes], mixed_out.at[c, :, lanes], mix_sem.at[c, h]
        )

    def fill(c, h):
        base = c * 6 + h * 3
        lanes = pl.ds(pl.multiple_of(h * DH, DH), DH)
        unit = unit_rows(qv[c, :, lanes])
        gate = dot(unit, w16[base])
        up = dot(unit, w16[base + 1])
        hidden = (gate * jax.nn.sigmoid(gate) * up).astype(BF16)
        recall[...] = dot(hidden, w16[base + 2])

        @pl.when(h == 0)
        def _():
            halo_copy(0, c).wait_recv()
            halo_copy(1, c).wait_recv()

        hc = jnp.maximum(c - first.astype(jnp.int32), 0)
        bias = jnp.where(jnp.logical_and(first, c == 0), -1e30, 0.0)
        for a in range(4):
            part = pl.ds(pl.multiple_of(h * DH + a * HEAD_DIM, HEAD_DIM), HEAD_DIM)
            query = qv[c, :, part]
            here = dot(query, kv[c, :, part], ((1,), (1,)))
            there = dot(query, halo[0, hc, :, part], ((1,), (1,)))
            scale = HEAD_DIM ** (-0.5)
            scores = jnp.where(near, here * scale, there * scale + bias)
            top = jnp.max(scores, axis=-1, keepdims=True)
            expo = jnp.exp(scores - top)
            probs = expo / jnp.sum(expo, axis=-1, keepdims=True)
            near_probs = jnp.where(near, probs, 0.0).astype(BF16)
            far_probs = jnp.where(near, 0.0, probs).astype(BF16)
            result = dot(near_probs, vv[c, :, part]) + dot(far_probs, halo[1, hc, :, part])
            local = pl.ds(a * HEAD_DIM, HEAD_DIM)
            mix[c, :, part] = (recall[:, local] + result).astype(BF16)
        mix_copy(c, h).start()

    def stage_h(c):
        halo_copy(0, c).start()
        halo_copy(1, c).start()

    stages = {
        "A": stage_a, "B1": stage_b1, "B2": stage_b2, "C1": stage_c1, "C2": stage_c2,
        "D": stage_d, "NA": stage_na, "NB": stage_nb, "E": stage_e, "H": stage_h,
        "F": lambda f: fill(lax.div(f, 2), lax.rem(f, 2)),
    }

    def body(i, carry):
        words, units = carry
        later_words, later_units = [], []
        for (name, plan), word, unit in zip(PLAN, words, units):
            for n in range(1, len(plan)):
                word = jnp.where(i == 30 * n, plan[n], word)
            bit = lax.rem(word, 2)

            @pl.when(bit == 1)
            def _(name=name, unit=unit):
                stages[name](unit)

            later_words.append(lax.div(word, 2))
            later_units.append(unit + bit)
        return tuple(later_words), tuple(later_units)

    start_words = tuple(jnp.int32(plan[0]) for _, plan in PLAN)
    lax.fori_loop(0, STEPS, body, (start_words, (jnp.int32(0),) * len(PLAN)))

    @pl.loop(0, 6)
    def _(i):
        w_send(i).wait_send()
        for copy in out_copies(i):
            copy.wait()

    @pl.loop(0, 3)
    def _(t):
        m_remote(t).wait_send()

    for c in range(2):
        halo_copy(0, c).wait_send()
        halo_copy(1, c).wait_send()
        for h in range(2):
            mix_copy(c, h).wait()


def shards(queries, keys, values, token_lr, momentum_rate, update_step, fast_weights, momentum):
    hbm = pl.BlockSpec(memory_space=pl.ANY)
    vmem = pl.BlockSpec(memory_space=pltpu.VMEM)
    smem = pl.BlockSpec(memory_space=pltpu.SMEM)
    dma = pltpu.SemaphoreType.DMA
    return pl.pallas_call(
        kernel,
        out_shape=(
            jax.ShapeDtypeStruct(queries.shape, BF16),
            jax.ShapeDtypeStruct(fast_weights.shape, F32),
            jax.ShapeDtypeStruct(momentum.shape, F32),
        ),
        in_specs=[hbm, hbm, hbm, vmem, smem, smem, hbm, hbm],
        out_specs=(hbm, hbm, hbm),
        scratch_shapes=[
            pltpu.VMEM((2, T, 1024), BF16),
            pltpu.VMEM((2, T, 1024), BF16),
            pltpu.VMEM((2, T, 1024), BF16),
            pltpu.VMEM((2, 2, T, 1024), BF16),
            pltpu.VMEM((2, T, 1024), BF16),
            pltpu.VMEM((T, DH), F32),
            pltpu.VMEM((6, DH, DH), F32),
            pltpu.VMEM((6, DH, DH), F32),
            pltpu.VMEM((12, DH, DH), BF16),
            pltpu.VMEM((3, T, DH), BF16),
            pltpu.VMEM((3, T, DH), BF16),
            pltpu.VMEM((2, T, DH), BF16),
            pltpu.VMEM((3, T, DH), BF16),
            pltpu.VMEM((6, T, DH), BF16),
            pltpu.VMEM((UNITS, T, DH), BF16),
            pltpu.VMEM((6, T, DH), F32),
            pltpu.VMEM((6, T, DH), BF16),
            pltpu.VMEM((UNITS, 192, DH), BF16),
            pltpu.VMEM((6, 128, DH), BF16),
            pltpu.VMEM((UNITS, 96, DH), BF16),
            pltpu.VMEM((UNITS, DH, DH), BF16),
            pltpu.VMEM((DH, DH), BF16),
            pltpu.VMEM((DH, DH), F32),
            pltpu.VMEM((DH, DH), BF16),
            pltpu.VMEM((DH, DH), BF16),
            pltpu.VMEM((6, T, DH), BF16),
            pltpu.VMEM((UNITS, T, DH), BF16),
            pltpu.VMEM((6, 8, DH), F32),
            pltpu.VMEM((UNITS, 8, DH), F32),
            dma((3,)), dma((6,)), dma((6,)), dma((6,)), dma((6,)), dma((3,)), dma((3,)),
            dma((2, 2)), dma((2, 2)),
            dma((9, UNITS)), dma((9, UNITS)), dma((2, 6)), dma((2, 2)),
        ],
        compiler_params=pltpu.CompilerParams(
            collective_id=0, has_side_effects=True, vmem_limit_bytes=66_000_000
        ),
    )(queries, keys, values, token_lr, momentum_rate, update_step, fast_weights, momentum)


def solution(mesh):
    wide = P(None, ("tok", "row"), "mem")
    state = P("mem", None, "row", None)
    return jax.shard_map(
        shards,
        mesh=mesh,
        in_specs=(wide, wide, wide, P("mem", None, ("tok", "row")), P("mem"), P("mem"), state, state),
        out_specs=(wide, state, state),
        check_vma=False,
    )
```

time: 138 us -> 120 us (0.87)
  Pallas kernels: 128 us -> 110 us
    pallas_call x1, Pallas kernels: 128 us -> 110 us  [shards(): pl.pallas_call(kernel, out_shape=(jax.ShapeDtypeStruct(queries.shape, BF1...]
where the time goes in v2:
time: 120 us; the launch traced here: 119 us
  Pallas kernels  110 us (92%)
  local copies, waits for them, and re-layouts  8.21 us (7%)
    pallas_call x1, Pallas kernels, shards(): pl.pallas_call(kernel, out_shape=(jax.ShapeDtypeStruct(queries.shape, BF1...  110 us
    unnamed x5, local copies, waits for them, and re-layouts  8.21 us

profile of v2, /device:TPU:1, one launch (start us, length us, event | category | flops | bytes accessed | tf_op | source)
XLA Modules:
  0.0 119.3 jit_solution(4092431940043109838)
XLA Ops:
  0.6 110.5 %shard_map.103 = (bf16[2,256,1024]{2,1,0:T(8,128)(2,1)}, f32[2,3,256,512]{3,2,1,0:T(8,128)}, f32[2,3,256,512]{3,2,1,0:T(8,128)}) custom-call(bf16[2,256,1024]{2,1,0:T(8,128)(2,1)} %q_in.1, bf16[2,256,1024]{2,1,0:T(8,128)(2,1)} %k_in.1, bf16[2,256,1024]{2,1,0:T(8,128)(2,1)} %v_in.1, f32[2,2,256]{2,1,0:T(2,128)} %lr_in.1, f32[2]{0:T(128)} %rate_in.1, ...), custom_call_target="tpu_custom_call" | custom-call | tf_op jit(solution)/shard_map/pallas_call | solution.py:533
  111.1 2.3 %copy.14 = bf16[2,256,1024]{2,1,0:T(8,128)(2,1)} copy(bf16[2,256,1024]{2,1,0:T(8,128)(2,1)} %get-tuple-element.6) | data formatting | bytes 2097152
  113.4 0.0 copy-start
  113.4 4.3 %copy.15 = f32[2,3,256,512]{3,2,1,0:T(8,128)} copy(f32[2,3,256,512]{3,2,1,0:T(8,128)} %get-tuple-element.7) | data formatting | bytes 6291456
  117.7 0.0 copy-done
  117.7 1.7 %copy.16 = f32[2,3,256,512]{3,2,1,0:T(8,128)} copy(f32[2,3,256,512]{3,2,1,0:T(8,128)S(1)} %copy-done) | data formatting | bytes 6291456
Async XLA Ops:
  113.4 4.3 %copy-start = (f32[2,3,256,512]{3,2,1,0:T(8,128)S(1)}, f32[2,3,256,512]{3,2,1,0:T(8,128)}, u32[]{:S(2)}) copy-start(f32[2,3,256,512]{3,2,1,0:T(8,128)} %get-tuple-element.8) | copy-start | bytes 9437188

commit v3 on v2

--- a/solution.py
+++ b/solution.py
@@ -13,23 +13,25 @@
 BF16 = jnp.bfloat16
 T = 256
 UNITS = 12
-ZC, XC = 384, 128
+ZC, XC = 256, 256
 ROWS_1 = (128 * ZC + 192 * XC) // DH
 ROWS_2 = (96 * ZC + 32 * XC) // DH
 
-STEPS = 59
+EARLY = 2
+STEPS = 53
 PLAN = (
-    ("H", (16777217, 0,)),
-    ("A", (805306927, 226,)),
-    ("B1", (4217, 1811,)),
-    ("B2", (69056, 23200,)),
-    ("F", (36864, 5120,)),
-    ("C2", (10919936, 710656,)),
-    ("D", (107282432, 6660096,)),
-    ("C1", (619008, 56832,)),
-    ("NA", (563347456, 14237697,)),
-    ("NB", (581435392, 15368193,)),
-    ("E", (234881024, 528482318,)),
+    ("A", (629145815, 5,)),
+    ("B1", (352322364, 26,)),
+    ("F", (4608, 40,)),
+    ("C1", (56576, 2637,)),
+    ("B2", (671094672, 170,)),
+    ("M", (128, 0,)),
+    ("C2", (483840, 21076,)),
+    ("NB", (56164352, 477696,)),
+    ("D", (7114752, 107792,)),
+    ("H", (1310720, 0,)),
+    ("E", (240386048, 8130560,)),
+    ("NA", (26886144, 221824,)),
 )
 
 
@@ -45,11 +47,11 @@
 def kernel(
     q_in, k_in, v_in, lr_in, rate_in, step_in, w_in, m_in,
     mixed_out, w_out, m_out,
-    qv, kv, vv, halo, mix, recall, w32, m32, w16, m_send, m_recv,
+    qv, kv, vv, halo, recall, w32, m32, w16, m_send, m_recv,
     left, right, send_a, recv_a, own, send_b, recv_b1, send_b2, recv_b2, total,
     ortho, gram, gram16, poly, x_send, x_recv, s_send, s_recv,
     load_sem, w_load, m_load, w_ssem, w_rsem, m_ssem, m_rsem, h_ssem, h_rsem,
-    ssem, rsem, out_sem, mix_sem,
+    ssem, rsem,
 ):
     tok = lax.axis_index("tok")
     row = lax.axis_index("row")
@@ -131,6 +133,9 @@
             source.at[c], halo.at[which, c], h_ssem.at[which, c], h_rsem.at[which, c], next_dev
         )
 
+    for n in range(EARLY):
+        halo_copy(n % 2, n // 2).start()
+
     @pl.loop(0, 6)
     def _(i):
         w_copy(i).wait()
@@ -139,16 +144,6 @@
 
     k_copy.wait()
     v_copy.wait()
-
-    @pl.loop(0, 6)
-    def _(i):
-        m_copy(i).wait()
-
-    @pl.loop(0, 3)
-    def _(t):
-        m_send[t] = m32[matrix(2 * t + other), pl.ds(mine, T)].astype(BF16)
-        m_remote(t).start()
-
     q_copy.wait()
 
     def split(u):
@@ -156,7 +151,7 @@
         m = lax.rem(u, 6)
         h = lax.div(m, 3)
         jj = lax.rem(m, 3)
-        return c, h, jj, matrix(m), m
+        return c, h, lax.rem(jj + 2, 3), matrix(m), m
 
     row_id = lax.broadcasted_iota(jnp.int32, (T, T), 0)
     col_id = lax.broadcasted_iota(jnp.int32, (T, T), 1)
@@ -195,7 +190,8 @@
         def _():
             keys(u)
 
-        _, _, jj, _, m = split(u)
+        m = lax.rem(u, 6)
+        jj = lax.rem(m, 3)
         li = jnp.minimum(jj, 1)
         rhs = right[jj]
         send_a[m] = dot(left[li, :, pl.ds(theirs, T)], rhs, ((0,), (0,))).astype(BF16)
@@ -289,13 +285,6 @@
         def _():
             d_copy(u).start()
 
-    def out_copies(i):
-        h, j = lax.div(i, 3), lax.rem(i, 3)
-        return (
-            pltpu.make_async_copy(w32.at[i, pl.ds(mine, T)], w_out.at[h, j], out_sem.at[0, i]),
-            pltpu.make_async_copy(m32.at[i, pl.ds(mine, T)], m_out.at[h, j], out_sem.at[1, i]),
-        )
-
     def newton_schulz():
         for b in range(4):
             rows = pl.ds(b * 128, 128)
@@ -313,7 +302,7 @@
             ortho[rows] = (QUINTIC[0] * old.astype(F32) + turned).astype(BF16)
 
     def stage_na(u):
-        c, h, _, i, m = split(u)
+        c, h, j, i, m = split(u)
         rate = rate_in[h]
 
         @pl.when(handles(u))
@@ -336,12 +325,22 @@
             for b in range(4):
                 rows = pl.ds(b * 128, 128)
                 ortho[rows] = (m32[i, rows] * inverse).astype(BF16)
+
+            @pl.when(c == 1)
+            def _():
+                m_out[h, j] = m32[i, pl.ds(mine, T)]
+
             newton_schulz()
 
         @pl.when(jnp.logical_not(handles(u)))
         def _():
             rows = pl.ds(mine, T)
-            m32[i, rows] = rate * m32[i, rows] + total[u, rows].astype(F32)
+            moment = rate * m32[i, rows] + total[u, rows].astype(F32)
+            m32[i, rows] = moment
+
+            @pl.when(c == 1)
+            def _():
+                m_out[h, j] = moment
 
     def x_copy(u):
         return remote(
@@ -358,7 +357,7 @@
         return remote(block, block, ssem.at[8, u], rsem.at[8, u], partner)
 
     def stage_nb(u):
-        c, h, _, i, m = split(u)
+        c, h, j, i, m = split(u)
 
         @pl.when(handles(u))
         def _():
@@ -393,13 +392,10 @@
 
             @pl.when(c == 1)
             def _():
-                rows = pl.ds(mine, T)
-                w32[i, rows] = w32[i, rows] * scale
-                for copy in out_copies(i):
-                    copy.start()
+                w_out[h, j] = w32[i, pl.ds(mine, T)] * scale
 
     def stage_e(u):
-        c, h, _, i, m = split(u)
+        c, h, j, i, m = split(u)
 
         @pl.when(jnp.logical_not(handles(u)))
         def _():
@@ -408,17 +404,16 @@
             rows = pl.ds(mine, T)
             scale = s_recv[u, pl.ds(0, 1), :]
             scaled = (w32[i, rows] - step_in[h] * x_recv[u].astype(F32)) * scale
-            w32[i, rows] = scaled
 
             @pl.when(c == 0)
             def _():
+                w32[i, rows] = scaled
                 w16[6 + i, rows] = scaled.astype(BF16)
                 half_copy(u, i, theirs).wait_recv()
 
             @pl.when(c == 1)
             def _():
-                for copy in out_copies(i):
-                    copy.start()
+                w_out[h, j] = scaled
 
             d_copy(u).wait_send()
 
@@ -439,12 +434,6 @@
 
     first = device == 0
     near = col_id <= row_id
-
-    def mix_copy(c, h):
-        lanes = pl.ds(pl.multiple_of(h * DH, DH), DH)
-        return pltpu.make_async_copy(
-            mix.at[c, :, lanes], mixed_out.at[c, :, lanes], mix_sem.at[c, h]
-        )
 
     def fill(c, h):
         base = c * 6 + h * 3
@@ -476,16 +465,32 @@
             far_probs = jnp.where(near, 0.0, probs).astype(BF16)
             result = dot(near_probs, vv[c, :, part]) + dot(far_probs, halo[1, hc, :, part])
             local = pl.ds(a * HEAD_DIM, HEAD_DIM)
-            mix[c, :, part] = (recall[:, local] + result).astype(BF16)
-        mix_copy(c, h).start()
-
-    def stage_h(c):
-        halo_copy(0, c).start()
-        halo_copy(1, c).start()
+            mixed_out[c, :, part] = (recall[:, local] + result).astype(BF16)
+
+    def stage_h(n):
+        c = lax.div(n, 2)
+
+        @pl.when(lax.rem(n, 2) == 0)
+        def _():
+            halo_copy(0, c).start()
+
+        @pl.when(lax.rem(n, 2) == 1)
+        def _():
+            halo_copy(1, c).start()
+
+    def stage_m(_):
+        @pl.loop(0, 6)
+        def _(i):
+            m_copy(i).wait()
+
+        @pl.loop(0, 3)
+        def _(t):
+            m_send[t] = m32[matrix(2 * t + other), pl.ds(mine, T)].astype(BF16)
+            m_remote(t).start()
 
     stages = {
         "A": stage_a, "B1": stage_b1, "B2": stage_b2, "C1": stage_c1, "C2": stage_c2,
-        "D": stage_d, "NA": stage_na, "NB": stage_nb, "E": stage_e, "H": stage_h,
+        "D": stage_d, "NA": stage_na, "NB": stage_nb, "E": stage_e, "H": stage_h, "M": stage_m,
         "F": lambda f: fill(lax.div(f, 2), lax.rem(f, 2)),
     }
 
@@ -506,13 +511,12 @@
         return tuple(later_words), tuple(later_units)
 
     start_words = tuple(jnp.int32(plan[0]) for _, plan in PLAN)
-    lax.fori_loop(0, STEPS, body, (start_words, (jnp.int32(0),) * len(PLAN)))
+    starts = tuple(jnp.int32(EARLY if name == "H" else 0) for name, _ in PLAN)
+    lax.fori_loop(0, STEPS, body, (start_words, starts))
 
     @pl.loop(0, 6)
     def _(i):
         w_send(i).wait_send()
-        for copy in out_copies(i):
-            copy.wait()
 
     @pl.loop(0, 3)
     def _(t):
@@ -521,8 +525,6 @@
     for c in range(2):
         halo_copy(0, c).wait_send()
         halo_copy(1, c).wait_send()
-        for h in range(2):
-            mix_copy(c, h).wait()
 
 
 def shards(queries, keys, values, token_lr, momentum_rate, update_step, fast_weights, momentum):
@@ -533,18 +535,17 @@
     return pl.pallas_call(
         kernel,
         out_shape=(
-            jax.ShapeDtypeStruct(queries.shape, BF16),
-            jax.ShapeDtypeStruct(fast_weights.shape, F32),
-            jax.ShapeDtypeStruct(momentum.shape, F32),
+            pltpu.VMEM(queries.shape, BF16),
+            pltpu.VMEM(fast_weights.shape, F32),
+            pltpu.VMEM(momentum.shape, F32),
         ),
         in_specs=[hbm, hbm, hbm, vmem, smem, smem, hbm, hbm],
-        out_specs=(hbm, hbm, hbm),
+        out_specs=(vmem, vmem, vmem),
         scratch_shapes=[
             pltpu.VMEM((2, T, 1024), BF16),
             pltpu.VMEM((2, T, 1024), BF16),
             pltpu.VMEM((2, T, 1024), BF16),
             pltpu.VMEM((2, 2, T, 1024), BF16),
-            pltpu.VMEM((2, T, 1024), BF16),
             pltpu.VMEM((T, DH), F32),
             pltpu.VMEM((6, DH, DH), F32),
             pltpu.VMEM((6, DH, DH), F32),
@@ -571,10 +572,10 @@
             pltpu.VMEM((UNITS, 8, DH), F32),
             dma((3,)), dma((6,)), dma((6,)), dma((6,)), dma((6,)), dma((3,)), dma((3,)),
             dma((2, 2)), dma((2, 2)),
-            dma((9, UNITS)), dma((9, UNITS)), dma((2, 6)), dma((2, 2)),
+            dma((9, UNITS)), dma((9, UNITS)),
         ],
         compiler_params=pltpu.CompilerParams(
-            collective_id=0, has_side_effects=True, vmem_limit_bytes=66_000_000
+            collective_id=0, has_side_effects=True, vmem_limit_bytes=58_700_000
         ),
     )(queries, keys, values, token_lr, momentum_rate, update_step, fast_weights, momentum)
 

time: 120 us -> 103 us (0.86)
  Pallas kernels: 110 us -> 97.8 us
  local copies, waits for them, and re-layouts: 8.21 us -> 4.3 us
    pallas_call x1, Pallas kernels: 110 us -> 97.8 us  [shards(): pl.pallas_call(kernel, out_shape=(pltpu.VMEM(queries.shape, BF16), pltpu....]
    unnamed x5 -> x3, local copies, waits for them, and re-layouts: 8.21 us -> 4.3 us
where the time goes in v3:
time: 103 us
  Pallas kernels  97.8 us (95%)
  local copies, waits for them, and re-layouts  4.3 us (4%)
    pallas_call x1, Pallas kernels, shards(): pl.pallas_call(kernel, out_shape=(pltpu.VMEM(queries.shape, BF16), pltpu....  97.8 us
    unnamed x3, local copies, waits for them, and re-layouts  4.3 us

profile of v3, /device:TPU:1, one launch (start us, length us, event | category | flops | bytes accessed | tf_op | source)
XLA Modules:
  0.0 102.7 jit_solution(9307064498909965890)
XLA Ops:
  0.6 97.8 %shard_map.103 = (bf16[2,256,1024]{2,1,0:T(8,128)(2,1)S(1)}, f32[2,3,256,512]{3,2,1,0:T(8,128)S(1)}, f32[2,3,256,512]{3,2,1,0:T(8,128)S(1)}) custom-call(bf16[2,256,1024]{2,1,0:T(8,128)(2,1)} %q_in.1, bf16[2,256,1024]{2,1,0:T(8,128)(2,1)} %k_in.1, bf16[2,256,1024]{2,1,0:T(8,128)(2,1)} %v_in.1, f32[2,2,256]{2,1,0:T(2,128)} %lr_in.1, f32[2]{0:T(128)} %rate_in.1, ...), custom_call_target="tpu_custom_call" | custom-call | tf_op jit(solution)/shard_map/pallas_call | solution.py:535
  98.4 1.0 copy.14
  99.4 1.7 %copy.15 = f32[2,3,256,512]{3,2,1,0:T(8,128)} copy(f32[2,3,256,512]{3,2,1,0:T(8,128)S(1)} %get-tuple-element.4) | data formatting | bytes 6291456
  101.1 1.7 %copy.16 = f32[2,3,256,512]{3,2,1,0:T(8,128)} copy(f32[2,3,256,512]{3,2,1,0:T(8,128)S(1)} %get-tuple-element.5) | data formatting | bytes 6291456

commit v4 on v3

--- a/solution.py
+++ b/solution.py
@@ -17,21 +17,21 @@
 ROWS_1 = (128 * ZC + 192 * XC) // DH
 ROWS_2 = (96 * ZC + 32 * XC) // DH
 
-EARLY = 2
-STEPS = 53
+EARLY = 8
+STEPS = 59
 PLAN = (
-    ("A", (629145815, 5,)),
-    ("B1", (352322364, 26,)),
-    ("F", (4608, 40,)),
-    ("C1", (56576, 2637,)),
-    ("B2", (671094672, 170,)),
-    ("M", (128, 0,)),
-    ("C2", (483840, 21076,)),
-    ("NB", (56164352, 477696,)),
-    ("D", (7114752, 107792,)),
-    ("H", (1310720, 0,)),
-    ("E", (240386048, 8130560,)),
-    ("NA", (26886144, 221824,)),
+    ("E", (117440512, 521142314,)),
+    ("M", (131072, 0,)),
+    ("B2", (133056, 26646,)),
+    ("C2", (151343104, 873472,)),
+    ("A", (738197791, 608,)),
+    ("F", (8320, 5120,)),
+    ("D", (816087040, 7114752,)),
+    ("NA", (576847872, 14303233,)),
+    ("H", (152895488, 9,)),
+    ("B1", (939528316, 2432,)),
+    ("C1", (4279552, 90720,)),
+    ("NB", (816054272, 15532033,)),
 )
 
 
@@ -85,6 +85,10 @@
             device_id=target, device_id_type=MESH,
         )
 
+    barrier = pltpu.get_barrier_semaphore()
+    for target in (partner, x_peer(1), x_peer(2), x_peer(3), z_peer, next_dev, prev_dev):
+        pl.semaphore_signal(barrier, inc=1, device_id=target, device_id_type=MESH)
+
     def w_copy(i):
         return pltpu.make_async_copy(
             w_in.at[lax.div(i, 3), lax.rem(i, 3)], w32.at[i, pl.ds(mine, T)], w_load.at[i]
@@ -112,9 +116,6 @@
 
     q_copy.start()
 
-    barrier = pltpu.get_barrier_semaphore()
-    for target in (partner, x_peer(1), x_peer(2), x_peer(3), z_peer, next_dev, prev_dev):
-        pl.semaphore_signal(barrier, inc=1, device_id=target, device_id_type=MESH)
     pl.semaphore_wait(barrier, 7)
 
     def w_send(i):
@@ -127,14 +128,16 @@
     def matrix(m):
         return lax.div(m, 3) * 3 + lax.rem(lax.rem(m, 3) + 2, 3)
 
-    def halo_copy(which, c):
+    def halo_copy(n, which):
+        c = lax.div(n, 8)
         source = (k_in, v_in)[which]
+        rows = pl.ds(pl.multiple_of(lax.rem(lax.div(n, 2), 4) * 64, 64), 64)
         return remote(
-            source.at[c], halo.at[which, c], h_ssem.at[which, c], h_rsem.at[which, c], next_dev
+            source.at[c, rows], halo.at[which, c, rows], h_ssem.at[n], h_rsem.at[n], next_dev
         )
 
     for n in range(EARLY):
-        halo_copy(n % 2, n // 2).start()
+        halo_copy(jnp.int32(n), n % 2).start()
 
     @pl.loop(0, 6)
     def _(i):
@@ -446,8 +449,10 @@
 
         @pl.when(h == 0)
         def _():
-            halo_copy(0, c).wait_recv()
-            halo_copy(1, c).wait_recv()
+            @pl.loop(0, 4)
+            def _(n):
+                for which in range(2):
+                    halo_copy(c * 8 + 2 * n + which, which).wait_recv()
 
         hc = jnp.maximum(c - first.astype(jnp.int32), 0)
         bias = jnp.where(jnp.logical_and(first, c == 0), -1e30, 0.0)
@@ -468,15 +473,10 @@
             mixed_out[c, :, part] = (recall[:, local] + result).astype(BF16)
 
     def stage_h(n):
-        c = lax.div(n, 2)
-
-        @pl.when(lax.rem(n, 2) == 0)
-        def _():
-            halo_copy(0, c).start()
-
-        @pl.when(lax.rem(n, 2) == 1)
-        def _():
-            halo_copy(1, c).start()
+        for which in range(2):
+            @pl.when(lax.rem(n, 2) == which)
+            def _(which=which):
+                halo_copy(n, which).start()
 
     def stage_m(_):
         @pl.loop(0, 6)
@@ -500,13 +500,13 @@
         for (name, plan), word, unit in zip(PLAN, words, units):
             for n in range(1, len(plan)):
                 word = jnp.where(i == 30 * n, plan[n], word)
-            bit = lax.rem(word, 2)
+            bit = lax.bitwise_and(word, 1)
 
             @pl.when(bit == 1)
             def _(name=name, unit=unit):
                 stages[name](unit)
 
-            later_words.append(lax.div(word, 2))
+            later_words.append(lax.shift_right_logical(word, 1))
             later_units.append(unit + bit)
         return tuple(later_words), tuple(later_units)
 
@@ -522,9 +522,10 @@
     def _(t):
         m_remote(t).wait_send()
 
-    for c in range(2):
-        halo_copy(0, c).wait_send()
-        halo_copy(1, c).wait_send()
+    @pl.loop(0, 8)
+    def _(n):
+        for which in range(2):
+            halo_copy(2 * n + which, which).wait_send()
 
 
 def shards(queries, keys, values, token_lr, momentum_rate, update_step, fast_weights, momentum):
@@ -571,7 +572,7 @@
             pltpu.VMEM((6, 8, DH), F32),
             pltpu.VMEM((UNITS, 8, DH), F32),
             dma((3,)), dma((6,)), dma((6,)), dma((6,)), dma((6,)), dma((3,)), dma((3,)),
-            dma((2, 2)), dma((2, 2)),
+            dma((16,)), dma((16,)),
             dma((9, UNITS)), dma((9, UNITS)),
         ],
         compiler_params=pltpu.CompilerParams(

time: 103 us -> 97.9 us (0.950)
  Pallas kernels: 97.8 us -> 92.8 us
    pallas_call x1, Pallas kernels: 97.8 us -> 92.8 us  [shards(): pl.pallas_call(kernel, out_shape=(pltpu.VMEM(queries.shape, BF16), pltpu....]
where the time goes in v4:
time: 97.9 us; the launch traced here: 97.8 us
  Pallas kernels  92.8 us (95%)
  local copies, waits for them, and re-layouts  4.3 us (4%)
    pallas_call x1, Pallas kernels, shards(): pl.pallas_call(kernel, out_shape=(pltpu.VMEM(queries.shape, BF16), pltpu....  92.8 us
    unnamed x3, local copies, waits for them, and re-layouts  4.3 us

profile of v4, /device:TPU:1, one launch (start us, length us, event | category | flops | bytes accessed | tf_op | source)
XLA Modules:
  0.0 97.8 jit_solution(17910771265959729397)
XLA Ops:
  0.6 92.8 %shard_map.103 = (bf16[2,256,1024]{2,1,0:T(8,128)(2,1)S(1)}, f32[2,3,256,512]{3,2,1,0:T(8,128)S(1)}, f32[2,3,256,512]{3,2,1,0:T(8,128)S(1)}) custom-call(bf16[2,256,1024]{2,1,0:T(8,128)(2,1)} %q_in.1, bf16[2,256,1024]{2,1,0:T(8,128)(2,1)} %k_in.1, bf16[2,256,1024]{2,1,0:T(8,128)(2,1)} %v_in.1, f32[2,2,256]{2,1,0:T(2,128)} %lr_in.1, f32[2]{0:T(128)} %rate_in.1, ...), custom_call_target="tpu_custom_call" | custom-call | tf_op jit(solution)/shard_map/pallas_call | solution.py:536
  93.5 1.0 copy.14
  94.5 1.7 %copy.15 = f32[2,3,256,512]{3,2,1,0:T(8,128)} copy(f32[2,3,256,512]{3,2,1,0:T(8,128)S(1)} %get-tuple-element.4) | data formatting | bytes 6291456
  96.1 1.7 %copy.16 = f32[2,3,256,512]{3,2,1,0:T(8,128)} copy(f32[2,3,256,512]{3,2,1,0:T(8,128)S(1)} %get-tuple-element.5) | data formatting | bytes 6291456

commit v5 on v4

--- a/solution.py
+++ b/solution.py
@@ -18,20 +18,20 @@
 ROWS_2 = (96 * ZC + 32 * XC) // DH
 
 EARLY = 8
-STEPS = 59
+STEPS = 56
 PLAN = (
-    ("E", (117440512, 521142314,)),
-    ("M", (131072, 0,)),
-    ("B2", (133056, 26646,)),
-    ("C2", (151343104, 873472,)),
-    ("A", (738197791, 608,)),
-    ("F", (8320, 5120,)),
-    ("D", (816087040, 7114752,)),
-    ("NA", (576847872, 14303233,)),
-    ("H", (152895488, 9,)),
-    ("B1", (939528316, 2432,)),
-    ("C1", (4279552, 90720,)),
-    ("NB", (816054272, 15532033,)),
+    ("E", (58720256, 65077276,)),
+    ("D", (611352576, 1746944,)),
+    ("H", (93192192, 9,)),
+    ("NA", (560988160, 3563521,)),
+    ("A", (234881119, 112,)),
+    ("C1", (2243584, 14896,)),
+    ("F", (20480, 1280,)),
+    ("B2", (75648, 1806,)),
+    ("B1", (939526776, 224,)),
+    ("C2", (21082112, 92800,)),
+    ("NB", (611319808, 3842049,)),
+    ("M", (128, 0,)),
 )
 
 

time: 97.9 us -> 97.4 us (level)
  no operation moved by 1% of the time
where the time goes in v5:
time: 97.4 us; the launch traced here: 97.3 us
  Pallas kernels  92.3 us (95%)
  local copies, waits for them, and re-layouts  4.3 us (4%)
    pallas_call x1, Pallas kernels, shards(): pl.pallas_call(kernel, out_shape=(pltpu.VMEM(queries.shape, BF16), pltpu....  92.3 us
    unnamed x3, local copies, waits for them, and re-layouts  4.3 us

profile of v5, /device:TPU:1, one launch (start us, length us, event | category | flops | bytes accessed | tf_op | source)
XLA Modules:
  0.0 97.3 jit_solution(11731855221459873561)
XLA Ops:
  0.6 92.3 %shard_map.103 = (bf16[2,256,1024]{2,1,0:T(8,128)(2,1)S(1)}, f32[2,3,256,512]{3,2,1,0:T(8,128)S(1)}, f32[2,3,256,512]{3,2,1,0:T(8,128)S(1)}) custom-call(bf16[2,256,1024]{2,1,0:T(8,128)(2,1)} %q_in.1, bf16[2,256,1024]{2,1,0:T(8,128)(2,1)} %k_in.1, bf16[2,256,1024]{2,1,0:T(8,128)(2,1)} %v_in.1, f32[2,2,256]{2,1,0:T(2,128)} %lr_in.1, f32[2]{0:T(128)} %rate_in.1, ...), custom_call_target="tpu_custom_call" | custom-call | tf_op jit(solution)/shard_map/pallas_call | solution.py:536
  93.0 1.0 copy.14
  93.9 1.7 %copy.15 = f32[2,3,256,512]{3,2,1,0:T(8,128)} copy(f32[2,3,256,512]{3,2,1,0:T(8,128)S(1)} %get-tuple-element.4) | data formatting | bytes 6291456
  95.6 1.7 %copy.16 = f32[2,3,256,512]{3,2,1,0:T(8,128)} copy(f32[2,3,256,512]{3,2,1,0:T(8,128)S(1)} %get-tuple-element.5) | data formatting | bytes 6291456
